TPU v7x, 256 devices: a whole 4x4x8 slice. The times are simulated.
256 devices in a mesh: section: 2 (over core), block: 16 (over y, x), dp: 8 (over z).
Axes of the slice: x: 4, y: 4, z: 8, core: 2. Of those that a mesh axis runs over, the one named last changes fastest.
Arguments:
- embeds: bfloat16 [16, 4096, 1024], P('dp', 'block'), parts along dimension 0, may hold values from -4 to 4
- wide_in: bfloat16 [2, 1024, 2304], P('section'), may hold values from -0.1875 to 0.1875
- rate_in: bfloat16 [2, 1024, 32], P('section'), may hold values from -0.375 to 0.375
- kernel: float32 [2, 4, 2304], P('section'), may hold values from -3 to 3
- kernel_bias: float32 [2, 2304], P('section'), may hold values from -0.5 to 0.5
- step_bias: float32 [2, 32], P('section'), may hold values from -12 to -1
- decay_log: float32 [2, 32], P('section'), may hold values from -2.3 to -0.7
- skip_gain: float32 [2, 32], P('section'), may hold values from 0.5 to 1.5
- norm_gain: float32 [2, 1024], P('section'), may hold values from 0.5 to 1.5
- inner_gain: float32 [2, 2048], P('section'), may hold values from 0.25 to 1.75
- proj_out: bfloat16 [2, 2048, 1024], P('section'), may hold values from -0.09375 to 0.09375
Outputs:
- hiddens: bfloat16 [2, 16, 4096, 1024], P('section', 'dp', 'block'), parts along dimension 1
There are 8 independent parts, one for each index of `dp`. A program takes and returns all parts, laid end to end along the dimension named above; an argument that names none is the same for every part. Nothing has to cross between parts.
All inputs are finite; a program needn't handle non-finite values.
Results may differ from a plain program's by a relative error of at most 0.039.
Values may be sent and summed in bfloat16 or wider, within the bound.
A program may use at most 128 MiB of HBM per device.

v0:
```python
import jax
import jax.numpy as jnp
from jax import lax
from jax.sharding import PartitionSpec as P


def from_behind(block, axis, distance):
    devices = range(lax.axis_size(axis))
    route = [(i - distance, i) for i in devices if i - distance in devices]
    return lax.ppermute(block, axis, route)


def entering(x, axis, combine, identity):
    count, mine = (lax.axis_size(axis), lax.axis_index(axis))
    everything = jax.tree.map(
        lambda part, kind: lax.all_gather(part.astype(kind), axis), x, (jnp.bfloat16, jnp.bfloat16)
    )
    start = jax.tree.map(
        lambda part, zero: jnp.broadcast_to(jnp.asarray(zero, part.dtype), part.shape), x, identity
    )

    def hop(k, before):
        reached = k < mine
        new = combine(
            before, jax.tree.map(lambda part, own: part[k].astype(own.dtype), everything, x)
        )
        return jax.tree.map(lambda a, b: jnp.where(reached, a, b), new, before)

    return lax.fori_loop(0, count, hop, start)


def rms_scale(values, gain):
    return values * lax.rsqrt(jnp.mean(values * values, axis=-1, keepdims=True) + 1e-05) * gain


def combine(earlier, later):
    return (earlier[0] * later[0], later[0][:, None, None] * earlier[1] + later[1])


def layer_apply(params, resid, valid):
    (
        weight_in,
        weight_rate,
        taps_weight,
        taps_bias,
        bias_step,
        decay_log,
        skip_head,
        gain_in,
        gain_inner,
        weight_out,
    ) = params
    rate = jnp.exp(decay_log)
    tokens, width = resid.shape
    heads = bias_step.shape[0]
    inner = weight_out.shape[0]
    head_size = inner // heads
    xbc_width = weight_in.shape[1]
    nstate = (xbc_width - inner) // 2
    taps = taps_weight.shape[0]
    positions = jnp.arange(tokens)
    causal = positions[:, None] >= positions[None, :]

    def front(resid):
        normed = rms_scale(resid.astype(jnp.float32), gain_in).astype(jnp.bfloat16)
        xbc_raw = jnp.dot(normed, weight_in, preferred_element_type=jnp.float32).astype(
            jnp.bfloat16
        )
        step_raw = jnp.dot(normed, weight_rate, preferred_element_type=jnp.float32)
        return (normed, xbc_raw, step_raw)

    def front_empty(resid):
        return (
            jnp.zeros((tokens, width), jnp.bfloat16),
            jnp.zeros((tokens, xbc_width), jnp.bfloat16),
            jnp.zeros((tokens, heads), jnp.float32),
        )

    def middle(xbc_raw, before, step_raw):
        padded = jnp.concatenate([before, xbc_raw], 0)
        convolved = taps_bias
        for offset in range(taps):
            convolved = (
                convolved
                + padded[offset : offset + tokens].astype(jnp.float32) * taps_weight[offset]
            )
        active = jax.nn.silu(convolved).astype(jnp.bfloat16)
        values = active[:, :inner]
        b_rows = active[:, inner : inner + nstate]
        c_rows = active[:, inner + nstate :]
        step = jax.nn.softplus(step_raw + bias_step)
        cumul = jnp.cumsum(-step * rate, axis=0).T
        gaps = cumul[:, :, None] - cumul[:, None, :]
        decay = jnp.where(causal[None], jnp.exp(jnp.where(causal[None], gaps, 0.0)), 0.0)
        scores = jnp.dot(c_rows, b_rows.T, preferred_element_type=jnp.float32)
        mixing = (scores[None] * decay * step.T[:, None, :]).astype(jnp.bfloat16)
        heads_view = values.reshape(tokens, heads, head_size)
        diagonal_part = jnp.einsum(
            "hij,jhp->ihp", mixing, heads_view, preferred_element_type=jnp.float32
        )
        tail_weight = jnp.exp(cumul[:, -1:] - cumul) * step.T
        weighted = (heads_view.astype(jnp.float32) * tail_weight.T[:, :, None]).astype(jnp.bfloat16)
        block_state = jnp.einsum(
            "ti,tn->in", weighted.reshape(tokens, inner), b_rows, preferred_element_type=jnp.float32
        ).reshape(heads, head_size, nstate)
        block_decay = jnp.exp(cumul[:, -1])
        return (
            values,
            c_rows,
            cumul,
            diagonal_part.reshape(tokens, inner),
            block_state,
            block_decay,
        )

    def middle_empty(xbc_raw, before, step_raw):
        return (
            jnp.zeros((tokens, inner), jnp.bfloat16),
            jnp.zeros((tokens, nstate), jnp.bfloat16),
            jnp.zeros((heads, tokens), jnp.float32),
            jnp.zeros((tokens, inner), jnp.float32),
            jnp.zeros((heads, head_size, nstate), jnp.float32),
            jnp.zeros((heads,), jnp.float32),
        )

    def back(resid, values, c_rows, cumul, diagonal_part, incoming):
        carried = jnp.einsum(
            "tn,in->ti",
            c_rows.astype(jnp.float32),
            incoming.reshape(inner, nstate),
            precision=lax.Precision.HIGHEST,
        )
        offdiag = carried.reshape(tokens, heads, head_size) * jnp.exp(cumul).T[:, :, None]
        skipped = (
            values.astype(jnp.float32).reshape(tokens, heads, head_size) * skip_head[None, :, None]
        )
        total = diagonal_part + (offdiag + skipped).reshape(tokens, inner)
        ynormed = rms_scale(total, gain_inner).astype(jnp.bfloat16)
        return (
            resid.astype(jnp.float32)
            + jnp.dot(ynormed, weight_out, preferred_element_type=jnp.float32)
        ).astype(jnp.bfloat16)

    def back_empty(resid, values, c_rows, cumul, diagonal_part, incoming):
        return jnp.zeros((tokens, width), jnp.bfloat16)

    normed, xbc_raw, step_raw = lax.cond(valid, front, front_empty, resid)
    before = from_behind(xbc_raw[tokens - (taps - 1) :], "block", 1)
    values, c_rows, cumul, diagonal_part, block_state, block_decay = lax.cond(
        valid, middle, middle_empty, xbc_raw, before, step_raw
    )
    scanned = entering(
        (block_decay, block_state),
        "block",
        combine,
        (jnp.ones_like(block_decay), jnp.zeros_like(block_state)),
    )
    incoming = scanned[1]
    return lax.cond(valid, back, back_empty, resid, values, c_rows, cumul, diagonal_part, incoming)


def shards(
    embeds,
    wide_in,
    rate_in,
    kernel,
    kernel_bias,
    step_bias,
    decay_log,
    skip_gain,
    norm_gain,
    inner_gain,
    proj_out,
):
    sections = lax.axis_size("section")
    section = lax.axis_index("section")
    seqs, tokens, width = embeds.shape
    params = (
        wide_in[0],
        rate_in[0],
        kernel[0],
        kernel_bias[0],
        step_bias[0],
        decay_log[0],
        skip_gain[0],
        norm_gain[0],
        inner_gain[0],
        proj_out[0],
    )
    ticks = seqs + sections - 1

    def tick(moment, carry):
        received, hiddens = carry
        micro = moment - section
        valid = (micro >= 0) & (micro < seqs)
        slot = jnp.clip(micro, 0, seqs - 1)
        fresh = lax.dynamic_index_in_dim(embeds, slot, 0, keepdims=False)
        resid = jnp.where(section == 0, fresh, received)
        result = layer_apply(params, resid, valid)
        hiddens = jnp.where(
            valid, lax.dynamic_update_index_in_dim(hiddens, result, slot, 0), hiddens
        )
        passed = from_behind(result, "section", 1)
        return (passed, hiddens)

    start = (
        jnp.zeros((tokens, width), jnp.bfloat16),
        jnp.zeros((seqs, tokens, width), jnp.bfloat16),
    )
    final, hiddens = lax.fori_loop(0, ticks, tick, start)
    return hiddens[None]


def solution(mesh):
    placed = (
        P("dp", "block", None),
        P("section", None, None),
        P("section", None, None),
        P("section", None, None),
        P("section", None),
        P("section", None),
        P("section", None),
        P("section", None),
        P("section", None),
        P("section", None),
        P("section", None, None),
    )
    return jax.shard_map(
        shards,
        mesh=mesh,
        in_specs=placed,
        out_specs=P("section", "dp", "block", None),
        check_vma=False,
    )
```

profile of v0, /device:TPU:249, one launch (start us, length us, event | category | flops | bytes accessed | tf_op | source)
XLA Modules:
  0.0 471.0 jit_solution(8303193776217909099)
XLA Ops:
  10.8 453.7 %while.50 = (s32[]{:T(128)}, bf16[256,1024]{1,0:T(8,128)(2,1)}, bf16[2,256,1024]{2,1,0:T(8,128)(2,1)}, s32[]{:T(128)}, pred[]{:T(512)}, /*index=5*/bf16[2,256,10...) while((s32[]{:T(128)}, bf16[256,1024]{1,0:T(8,128)(2,1)}, ...), condition=%wide.region_13.14_spmd, body=%wide.region_0.13_spmd.sunk | while | flops 3565380608 | bytes 128007672 | solution.py:210
  20.4 4.3 conditional.7
  27.6 24.2 %all-reduce.2 = bf16[512]{0:T(512)(128)(2,1)S(1)} all-reduce(bf16[512]{0:T(512)(128)(2,1)S(1)} %dynamic-update-slice.7), channel_id=2, replica_groups=mesh['section'=2,'block'=16,'dp'=8] {'block'}, use_global_device_ids=true, to_apply=%add | all-reduce | flops 512 | bytes 2048 | tf_op jit(solution)/shard_map/while
  51.9 74.2 %all-gather.6.cloned.1.call-done = bf16[512,64,128]{2,1,0:T(8,128)(2,1)} async-done(((bf16[32,64,128]{2,1,0:T(8,128)(2,1)}), bf16[512,64,128]{2,1,0:T(8,128)(2,1)}) %all-gather.6.cloned.1.call-update) | async-done | bytes 8388624 | tf_op jit(solution)/shard_map/while/body/eval_jaxpr/all_gather | solution.py:16
  126.2 21.4 %while.51 = (s32[]{:T(128)}, f32[32,64,128]{2,1,0:T(8,128)S(1)}, s32[]{:T(128)}, bf16[16,32]{1,0:T(8,128)(2,1)S(1)}, bf16[16,32,64,128]{3,2,1,0:T(8,128)(2,1)}, /*index=5*/s32[]{:T(128)}, s32[]{:T(128)}) while((s32[]{:T(128)}, f32[32,64,128]{2,1,0:T(8,128)S(1)}, s32[]{:T(128)}, bf16[16,32]{1,0:T(8,128)(2,1)S(1)}, ...), condition=%wide.region_9.9_spmd.clone, body=%wide.region_8.8_spmd.clone.sunk | while | flops 1310756 | bytes 2621865 | solution.py:29
  151.9 9.8 %collective-permute-done.1 = bf16[256,1024]{1,0:T(8,128)(2,1)} collective-permute-done((bf16[256,1024]{1,0:T(8,128)(2,1)}, bf16[256,1024]{1,0:T(8,128)(2,1)}, u32[]{:S(2)}, u32[]{:S(2)}) %collective-permute-start.1) | collective-permute-done | bytes 524320 | tf_op jit(solution)/shard_map/while/body/eval_jaxpr/ppermute | solution.py:10
  163.8 6.7 %conditional.6 = (bf16[256,2304]{1,0:T(8,128)(2,1)S(1)}, f32[256,32]{0,1:T(8,128)S(1)}) conditional(s32[]{:T(128)} %convert_element_type.139, () %tuple.112, (bf16[256,1024]{1,0:T(8,128)(2,1)}, f32[1,1024]{1,0:T(1,128)}, bf16[1024,2304]{1,0:T(8,128)(2,1)}, bf16[1024,32]{1,0:T(8,128)(2,1)}) %tuple.113), branch_computations={%region_1.1_spmd, %region_2.3_spmd} | conditional | flops 1228210432 | bytes 7599148 | solution.py:147
  165.0 4.0 convolution_convert_fusion
  172.4 4.7 collective-permute-done
  177.9 24.0 %conditional.7 = (bf16[256,2048]{1,0:T(8,128)(2,1)S(1)}, bf16[256,128]{1,0:T(8,128)(2,1)}, f32[32,256]{1,0:T(8,128)}, f32[256,2048]{0,1:T(8,128)}, bf16[32,64,128]{2,1,0:T(8,128)(2,1)}, /*index=5*/bf16[32]{0:T(256)(128)(2,1)}) conditional(s32[]{:T(128)} %convert_element_type.139, () %tuple.111, (f32[1,2304]{1,0:T(1,128)S(1)}, ...), branch_computations={%region_4.4_spmd, %region_5.7_spmd} | conditional | flops 450257024 | bytes 47047460 | solution.py:149
  192.5 5.1 %fusion.12 = f32[32,64,256]{2,1,0:T(8,128)} fusion(bf16[256,32,64]{0,2,1:T(8,128)(2,1)} %bitcast.83, f32[32,256]{1,0:T(8,128)} %get-tuple-element.663, f32[32,256]{1,0:T(8,128)} %copy_bitcast_fusion, f32[256,256]{1,0:T(8,128)S(1)} %fusion.26, pred[256,256]{1,0:T(8,128)(4,1)S(1)} %ge.40, pred[256,256]{1,0:T(8,128)(4,1)S(1)} %ge.39), kind=kOutput, calls=%fused_computation.24 | convolution fusion | flops 281018368 | bytes 3604480 | tf_op jit(solution)/shard_map/while/body/eval_jaxpr/cond/branch_1_fun/hij,jhp->ihp/dot_general | solution.py:98
  204.8 24.0 %all-reduce.2 = bf16[512]{0:T(512)(128)(2,1)S(1)} all-reduce(bf16[512]{0:T(512)(128)(2,1)S(1)} %dynamic-update-slice.7), channel_id=2, replica_groups=mesh['section'=2,'block'=16,'dp'=8] {'block'}, use_global_device_ids=true, to_apply=%add | all-reduce | flops 512 | bytes 2048 | tf_op jit(solution)/shard_map/while
  228.8 49.4 %all-gather.6.cloned.1.call-done = bf16[512,64,128]{2,1,0:T(8,128)(2,1)} async-done(((bf16[32,64,128]{2,1,0:T(8,128)(2,1)}), bf16[512,64,128]{2,1,0:T(8,128)(2,1)}) %all-gather.6.cloned.1.call-update) | async-done | bytes 8388624 | tf_op jit(solution)/shard_map/while/body/eval_jaxpr/all_gather | solution.py:16
  278.3 21.4 %while.51 = (s32[]{:T(128)}, f32[32,64,128]{2,1,0:T(8,128)S(1)}, s32[]{:T(128)}, bf16[16,32]{1,0:T(8,128)(2,1)S(1)}, bf16[16,32,64,128]{3,2,1,0:T(8,128)(2,1)}, /*index=5*/s32[]{:T(128)}, s32[]{:T(128)}) while((s32[]{:T(128)}, f32[32,64,128]{2,1,0:T(8,128)S(1)}, s32[]{:T(128)}, bf16[16,32]{1,0:T(8,128)(2,1)S(1)}, ...), condition=%wide.region_9.9_spmd.clone, body=%wide.region_8.8_spmd.clone.sunk | while | flops 1310756 | bytes 2621865 | solution.py:29
  299.7 10.3 %conditional.8 = (bf16[256,1024]{1,0:T(8,128)(2,1)}, bf16[1,256,1024]{2,1,0:T(8,128)(2,1)S(1)}) conditional(s32[]{:T(128)} %convert_element_type.139, () %tuple.110, (bf16[256,1024]{1,0:T(8,128)(2,1)}, bf16[256,128]{1,0:T(8,128)(2,1)}, f32[32,64,128]{2,1,0:T(8,128)S(1)}, f32[32,256]{1,0:T(8,128)}, bf16[256,2048]{1,0:T(8,128)(2,1)S(1)}, ...), branch_computations={%region_10.10_spmd, %region_11.12_spmd} | conditional | flops 1885077760 | bytes 37925036 | solution.py:159
  316.3 6.7 %conditional.6 = (bf16[256,2304]{1,0:T(8,128)(2,1)S(1)}, f32[256,32]{0,1:T(8,128)S(1)}) conditional(s32[]{:T(128)} %convert_element_type.139, () %tuple.112, (bf16[256,1024]{1,0:T(8,128)(2,1)}, f32[1,1024]{1,0:T(1,128)}, bf16[1024,2304]{1,0:T(8,128)(2,1)}, bf16[1024,32]{1,0:T(8,128)(2,1)}) %tuple.113), branch_computations={%region_1.1_spmd, %region_2.3_spmd} | conditional | flops 1228210432 | bytes 7599148 | solution.py:147
  317.5 4.0 convolution_convert_fusion
  324.9 4.7 collective-permute-done
  330.4 24.0 %conditional.7 = (bf16[256,2048]{1,0:T(8,128)(2,1)S(1)}, bf16[256,128]{1,0:T(8,128)(2,1)}, f32[32,256]{1,0:T(8,128)}, f32[256,2048]{0,1:T(8,128)}, bf16[32,64,128]{2,1,0:T(8,128)(2,1)}, /*index=5*/bf16[32]{0:T(256)(128)(2,1)}) conditional(s32[]{:T(128)} %convert_element_type.139, () %tuple.111, (f32[1,2304]{1,0:T(1,128)S(1)}, ...), branch_computations={%region_4.4_spmd, %region_5.7_spmd} | conditional | flops 450257024 | bytes 47047460 | solution.py:149
  345.0 5.1 %fusion.12 = f32[32,64,256]{2,1,0:T(8,128)} fusion(bf16[256,32,64]{0,2,1:T(8,128)(2,1)} %bitcast.83, f32[32,256]{1,0:T(8,128)} %get-tuple-element.663, f32[32,256]{1,0:T(8,128)} %copy_bitcast_fusion, f32[256,256]{1,0:T(8,128)S(1)} %fusion.26, pred[256,256]{1,0:T(8,128)(4,1)S(1)} %ge.40, pred[256,256]{1,0:T(8,128)(4,1)S(1)} %ge.39), kind=kOutput, calls=%fused_computation.24 | convolution fusion | flops 281018368 | bytes 3604480 | tf_op jit(solution)/shard_map/while/body/eval_jaxpr/cond/branch_1_fun/hij,jhp->ihp/dot_general | solution.py:98
  357.2 24.1 %all-reduce.2 = bf16[512]{0:T(512)(128)(2,1)S(1)} all-reduce(bf16[512]{0:T(512)(128)(2,1)S(1)} %dynamic-update-slice.7), channel_id=2, replica_groups=mesh['section'=2,'block'=16,'dp'=8] {'block'}, use_global_device_ids=true, to_apply=%add | all-reduce | flops 512 | bytes 2048 | tf_op jit(solution)/shard_map/while
  381.4 47.2 %all-gather.6.cloned.1.call-done = bf16[512,64,128]{2,1,0:T(8,128)(2,1)} async-done(((bf16[32,64,128]{2,1,0:T(8,128)(2,1)}), bf16[512,64,128]{2,1,0:T(8,128)(2,1)}) %all-gather.6.cloned.1.call-update) | async-done | bytes 8388624 | tf_op jit(solution)/shard_map/while/body/eval_jaxpr/all_gather | solution.py:16
  428.6 21.4 %while.51 = (s32[]{:T(128)}, f32[32,64,128]{2,1,0:T(8,128)S(1)}, s32[]{:T(128)}, bf16[16,32]{1,0:T(8,128)(2,1)S(1)}, bf16[16,32,64,128]{3,2,1,0:T(8,128)(2,1)}, /*index=5*/s32[]{:T(128)}, s32[]{:T(128)}) while((s32[]{:T(128)}, f32[32,64,128]{2,1,0:T(8,128)S(1)}, s32[]{:T(128)}, bf16[16,32]{1,0:T(8,128)(2,1)S(1)}, ...), condition=%wide.region_9.9_spmd.clone, body=%wide.region_8.8_spmd.clone.sunk | while | flops 1310756 | bytes 2621865 | solution.py:29
  450.1 10.3 %conditional.8 = (bf16[256,1024]{1,0:T(8,128)(2,1)}, bf16[1,256,1024]{2,1,0:T(8,128)(2,1)S(1)}) conditional(s32[]{:T(128)} %convert_element_type.139, () %tuple.110, (bf16[256,1024]{1,0:T(8,128)(2,1)}, bf16[256,128]{1,0:T(8,128)(2,1)}, f32[32,64,128]{2,1,0:T(8,128)S(1)}, f32[32,256]{1,0:T(8,128)}, bf16[256,2048]{1,0:T(8,128)(2,1)S(1)}, ...), branch_computations={%region_10.10_spmd, %region_11.12_spmd} | conditional | flops 1885077760 | bytes 37925036 | solution.py:159
  (295 shorter events, 174.4 us)
Async XLA Ops:
  10.8 115.3 %all-gather.6.cloned.1.call-start = ((), (), s32[]{:S(2)}) async-start(), calls=%async_computation | async-start | bytes 8912896 | tf_op jit(solution)/shard_map/while/body/eval_jaxpr/all_gather | solution.py:16
  13.0 6.6 %collective-permute-start = (bf16[3,2304]{1,0:T(4,128)(2,1)S(1)}, bf16[3,2304]{1,0:T(4,128)(2,1)S(1)}, u32[]{:S(2)}, u32[]{:S(2)}) collective-permute-start(bf16[3,2304]{1,0:T(4,128)(2,1)S(1)} %slice.84), channel_id=1, source_target_pairs={{0,8},{8,16},{16,24},{24,32},{32,40},{40,48},{48,56},{56,64},{64,7... | collective-permute-start | bytes 41480 | tf_op jit(solution)/shard_map/while/body/eval_jaxpr/ppermute | solution.py:10
  126.2 21.4 %copy-start.9 = (f32[1,32]{1,0:T(1,128)S(1)}, f32[1,32]{1,0:T(1,128)}, u32[]{:S(2)}) copy-start(f32[1,32]{1,0:T(1,128)} %get-tuple-element.935) | copy-start | bytes 388 | tf_op jit(solution)/shard_map/while
  126.2 21.4 %copy-start.13 = (f32[1,2048]{1,0:T(1,128)S(1)}, f32[1,2048]{1,0:T(1,128)}, u32[]{:S(2)}) copy-start(f32[1,2048]{1,0:T(1,128)} %get-tuple-element.936) | copy-start | bytes 24580 | tf_op jit(solution)/shard_map/while
  148.6 13.1 %collective-permute-start.1 = (bf16[256,1024]{1,0:T(8,128)(2,1)}, bf16[256,1024]{1,0:T(8,128)(2,1)}, u32[]{:S(2)}, u32[]{:S(2)}) collective-permute-start(bf16[256,1024]{1,0:T(8,128)(2,1)} %get-tuple-element.819), channel_id=1, source_target_pairs={{0,128},{1,129},{2,130},{3,131},{4,132},{5,133},{6,134},{7,135},{8... | collective-permute-start | bytes 1572872 | tf_op jit(solution)/shard_map/while/body/eval_jaxpr/ppermute | solution.py:10
  161.7 16.2 %copy-start.10 = (f32[32]{0:T(128)}, f32[32]{0:T(128)S(1)}, u32[]{:S(2)}) copy-start(f32[32]{0:T(128)S(1)} %get-tuple-element.934) | copy-start | bytes 388 | tf_op jit(solution)/shard_map/while
  161.7 116.6 %all-gather.6.cloned.1.call-start = ((), (), s32[]{:S(2)}) async-start(), calls=%async_computation | async-start | bytes 8912896 | tf_op jit(solution)/shard_map/while/body/eval_jaxpr/all_gather | solution.py:16
  163.8 14.1 %copy-start.4 = (f32[4,2304]{1,0:T(4,128)S(1)}, f32[4,2304]{1,0:T(4,128)}, u32[]{:S(2)}) copy-start(f32[4,2304]{1,0:T(4,128)} %get-tuple-element.932) | copy-start | bytes 110596 | tf_op jit(solution)/shard_map/while
  163.8 14.1 %copy-start.5 = (f32[1,2304]{1,0:T(1,128)S(1)}, f32[1,2304]{1,0:T(1,128)}, u32[]{:S(2)}) copy-start(f32[1,2304]{1,0:T(1,128)} %get-tuple-element.931) | copy-start | bytes 27652 | tf_op jit(solution)/shard_map/while
  163.8 14.1 %copy-start.6 = (f32[1,32]{1,0:T(1,128)S(1)}, f32[1,32]{1,0:T(1,128)}, u32[]{:S(2)}) copy-start(f32[1,32]{1,0:T(1,128)} %get-tuple-element.933) | copy-start | bytes 388 | tf_op jit(solution)/shard_map/while
  170.5 6.6 %collective-permute-start = (bf16[3,2304]{1,0:T(4,128)(2,1)S(1)}, bf16[3,2304]{1,0:T(4,128)(2,1)S(1)}, u32[]{:S(2)}, u32[]{:S(2)}) collective-permute-start(bf16[3,2304]{1,0:T(4,128)(2,1)S(1)} %slice.84), channel_id=1, source_target_pairs={{0,8},{8,16},{16,24},{24,32},{32,40},{40,48},{48,56},{56,64},{64,7... | collective-permute-start | bytes 41480 | tf_op jit(solution)/shard_map/while/body/eval_jaxpr/ppermute | solution.py:10
  278.3 21.4 %copy-start.9 = (f32[1,32]{1,0:T(1,128)S(1)}, f32[1,32]{1,0:T(1,128)}, u32[]{:S(2)}) copy-start(f32[1,32]{1,0:T(1,128)} %get-tuple-element.935) | copy-start | bytes 388 | tf_op jit(solution)/shard_map/while
  278.3 21.4 %copy-start.13 = (f32[1,2048]{1,0:T(1,128)S(1)}, f32[1,2048]{1,0:T(1,128)}, u32[]{:S(2)}) copy-start(f32[1,2048]{1,0:T(1,128)} %get-tuple-element.936) | copy-start | bytes 24580 | tf_op jit(solution)/shard_map/while
  299.7 14.5 %copy-start.11 = (f32[32]{0:T(128)S(1)}, f32[32]{0:T(128)}, u32[]{:S(2)}) copy-start(f32[32]{0:T(128)} %copy-done.10) | copy-start | bytes 388 | tf_op jit(solution)/shard_map/while
  310.0 4.1 collective-permute-start.1
  314.2 16.2 %copy-start.10 = (f32[32]{0:T(128)}, f32[32]{0:T(128)S(1)}, u32[]{:S(2)}) copy-start(f32[32]{0:T(128)S(1)} %get-tuple-element.934) | copy-start | bytes 388 | tf_op jit(solution)/shard_map/while
  314.2 114.4 %all-gather.6.cloned.1.call-start = ((), (), s32[]{:S(2)}) async-start(), calls=%async_computation | async-start | bytes 8912896 | tf_op jit(solution)/shard_map/while/body/eval_jaxpr/all_gather | solution.py:16
  316.3 14.1 %copy-start.5 = (f32[1,2304]{1,0:T(1,128)S(1)}, f32[1,2304]{1,0:T(1,128)}, u32[]{:S(2)}) copy-start(f32[1,2304]{1,0:T(1,128)} %get-tuple-element.931) | copy-start | bytes 27652 | tf_op jit(solution)/shard_map/while
  316.3 14.1 %copy-start.6 = (f32[1,32]{1,0:T(1,128)S(1)}, f32[1,32]{1,0:T(1,128)}, u32[]{:S(2)}) copy-start(f32[1,32]{1,0:T(1,128)} %get-tuple-element.933) | copy-start | bytes 388 | tf_op jit(solution)/shard_map/while
  323.0 6.6 %collective-permute-start = (bf16[3,2304]{1,0:T(4,128)(2,1)S(1)}, bf16[3,2304]{1,0:T(4,128)(2,1)S(1)}, u32[]{:S(2)}, u32[]{:S(2)}) collective-permute-start(bf16[3,2304]{1,0:T(4,128)(2,1)S(1)} %slice.84), channel_id=1, source_target_pairs={{0,8},{8,16},{16,24},{24,32},{32,40},{40,48},{48,56},{56,64},{64,7... | collective-permute-start | bytes 41480 | tf_op jit(solution)/shard_map/while/body/eval_jaxpr/ppermute | solution.py:10
  428.6 21.4 %copy-start.9 = (f32[1,32]{1,0:T(1,128)S(1)}, f32[1,32]{1,0:T(1,128)}, u32[]{:S(2)}) copy-start(f32[1,32]{1,0:T(1,128)} %get-tuple-element.935) | copy-start | bytes 388 | tf_op jit(solution)/shard_map/while
  428.6 21.4 %copy-start.13 = (f32[1,2048]{1,0:T(1,128)S(1)}, f32[1,2048]{1,0:T(1,128)}, u32[]{:S(2)}) copy-start(f32[1,2048]{1,0:T(1,128)} %get-tuple-element.936) | copy-start | bytes 24580 | tf_op jit(solution)/shard_map/while
  450.0 14.5 %copy-start.11 = (f32[32]{0:T(128)S(1)}, f32[32]{0:T(128)}, u32[]{:S(2)}) copy-start(f32[32]{0:T(128)} %copy-done.10) | copy-start | bytes 388 | tf_op jit(solution)/shard_map/while
  460.4 4.1 collective-permute-start.1
  (22 other events, 129.8 us)
Sparse Core Ops, SparseCore 0:
  24.9 101.2 all-gather.5
  202.0 76.1 all-gather.5
  354.5 74.0 all-gather.5
where the time goes:
time: 479 us; the launch traced here: 471 us
  waiting for transfers between devices  195 us (41%)
  other arithmetic  99.8 us (21%)
  blocking collectives  72.3 us (15%)
  matrix products  38.1 us (8%)
  local copies, waits for them, and re-layouts  37.5 us (8%)
  between operations  13.1 us (3%)
  starting transfers between devices  10.8 us (2%)
    all_gather x3, waiting for transfers between devices, entering(): lax.all_gather(part.astype(kind), axis)  171 us
    while x3, blocking collectives  72.3 us
    select_n x48, other arithmetic, hop(): return jax.tree.map(lambda a, b: jnp.where(reached, a, b), new, before)  62.4 us
    ppermute x6, waiting for transfers between devices, from_behind(): return lax.ppermute(block, axis, route)  24.2 us
    ppermute x6, starting transfers between devices, from_behind(): return lax.ppermute(block, axis, route)  10.8 us
    dot_general x2, matrix products, middle(): jnp.einsum('hij,jhp->ihp', mixing, heads_view, preferred_element_type=jnp...  10.1 us
  transfers between devices with their start and end apart: 9, of which 9 were waited for; matrix products, arithmetic and copies ran while one was open for 3% of the time, Pallas kernels for 0%

commit v1 on v0

v1 whole, which is shorter than its diff:
```python
import functools

import jax
import jax.numpy as jnp
from jax import lax
from jax.experimental import pallas as pl
from jax.experimental.pallas import tpu as pltpu
from jax.sharding import PartitionSpec as P

MESH = pl.DeviceIdType.MESH
F32, BF16 = jnp.float32, jnp.bfloat16
LOG2E = 1.4426950408889634
EPS = 1e-05
DECAY_ROWS = 16


def split2(x):
    hi = x.astype(BF16)
    return hi, (x - hi.astype(F32)).astype(BF16)


def dot(a, b):
    return jnp.dot(a, b, preferred_element_type=F32)


def dot_nt(a, b):
    return lax.dot_general(a, b, (((1,), (1,)), ((), ())), preferred_element_type=F32)


def kernel(
    blocks,
    emb, wide, rate, taps, tbias, sbias, dlog, skip, ngain, igain, proj,
    out,
    h, win, wo, rt, pp, tril, expand,
    xs, halo, act, scores, cum, rowt, total,
    msg, rcv, inco, inc, part, prec,
    local_sem, out_sem, wsend, wrecv, hsend, hrecv,
    msend, mrecv, isend, irecv, psend, precv, xsend, xrecv,
):
    core = lax.axis_index("section")
    me = lax.axis_index("block")
    other = 1 - core
    seqs, tokens, width = emb.shape
    half = wo.shape[1]
    bc = win.shape[2] - half
    nstate = bc // 2
    heads = msg.shape[2]
    head = half // heads
    inner = 2 * half
    rows = tokens // 2

    barrier = pltpu.get_barrier_semaphore()
    pl.semaphore_signal(barrier, inc=1, device_id={"section": other}, device_id_type=MESH)

    def greet(k, _):
        peer = lax.rem(me + k, blocks)
        pl.semaphore_signal(barrier, inc=1, device_id={"block": peer}, device_id_type=MESH)
        return 0

    lax.fori_loop(1, blocks, greet, 0)

    def half_at(which):
        return pl.ds(pl.multiple_of(which * half, half), half)

    loads = [
        pltpu.make_async_copy(emb, h.at[0], local_sem.at[0]),
        pltpu.make_async_copy(wide.at[0, :, half_at(core)], win.at[core, :, pl.ds(0, half)], local_sem.at[1]),
        pltpu.make_async_copy(wide.at[0, :, pl.ds(inner, bc)], win.at[core, :, pl.ds(half, bc)], local_sem.at[2]),
        pltpu.make_async_copy(proj.at[0, half_at(core), :], wo.at[core], local_sem.at[3]),
    ]
    for load in loads:
        load.start()

    pp[core, 0:4, :] = taps[0]
    pp[core, 4:5, :] = tbias[...]
    pp[core, 5:6, 0:width] = ngain[...]
    pp[core, 6:7, 0:inner] = igain[...]
    pp[core, 7:8, 0 : 2 * heads] = sbias[...]
    pp[core, 8:9, 0 : 2 * heads] = dlog[...]
    pp[core, 9:10, 0 : 2 * heads] = skip[...]
    rt[core] = rate[0]

    pl.semaphore_wait(barrier, blocks)

    def push(i, src, dst):
        return pltpu.make_async_remote_copy(
            src_ref=src, dst_ref=dst, send_sem=wsend.at[i], recv_sem=wrecv.at[i],
            device_id={"section": other}, device_id_type=MESH,
        )

    pushes = [
        push(0, wide.at[0, :, half_at(other)], win.at[core, :, pl.ds(0, half)]),
        push(1, wide.at[0, :, pl.ds(inner, bc)], win.at[core, :, pl.ds(half, bc)]),
        push(2, rt.at[core], rt.at[core]),
        push(3, pp.at[core], pp.at[core]),
        push(4, proj.at[0, half_at(other), :], wo.at[core]),
    ]
    for copy in pushes:
        copy.start()
    arrivals = [
        push(0, wide.at[0, :, half_at(core)], win.at[other, :, pl.ds(0, half)]),
        push(1, wide.at[0, :, pl.ds(inner, bc)], win.at[other, :, pl.ds(half, bc)]),
        push(2, rt.at[core], rt.at[other]),
        push(3, pp.at[core], pp.at[other]),
        push(4, proj.at[0, half_at(core), :], wo.at[other]),
    ]

    ri = lax.broadcasted_iota(jnp.int32, (tokens, tokens), 0)
    ci = lax.broadcasted_iota(jnp.int32, (tokens, tokens), 1)
    tril[...] = jnp.where(ri >= ci, 1.0, 0.0).astype(BF16)
    eh = lax.broadcasted_iota(jnp.int32, (heads, half), 0)
    ec = lax.broadcasted_iota(jnp.int32, (heads, half), 1)
    expand[...] = jnp.where((ec >= eh * head) & (ec < eh * head + head), 1.0, 0.0).astype(BF16)

    loads[0].wait()

    def mine(row):
        return jnp.where(core == 0, row[:, 0:heads], row[:, heads : 2 * heads])

    def halo_copy(l, s, peer):
        return pltpu.make_async_remote_copy(
            src_ref=xs.at[l, s, pl.ds(tokens, 8), :], dst_ref=halo.at[l, s],
            send_sem=hsend.at[l, s], recv_sem=hrecv.at[l, s],
            device_id={"block": peer}, device_id_type=MESH,
        )

    def state_copy(l, s, k):
        peer = lax.rem(me + k, blocks)
        return pltpu.make_async_remote_copy(
            src_ref=msg.at[l, s, peer], dst_ref=rcv.at[l, s, me],
            send_sem=msend.at[l, s, k], recv_sem=mrecv.at[l, s, me],
            device_id={"block": peer}, device_id_type=MESH,
        )

    def state_arrival(l, s, b):
        return pltpu.make_async_remote_copy(
            src_ref=msg.at[l, s, b], dst_ref=rcv.at[l, s, b],
            send_sem=msend.at[l, s, 0], recv_sem=mrecv.at[l, s, b],
            device_id={"block": b}, device_id_type=MESH,
        )

    def reply_copy(l, s, b):
        return pltpu.make_async_remote_copy(
            src_ref=inco.at[l, s, b], dst_ref=inc.at[l, s, me],
            send_sem=isend.at[l, s, b], recv_sem=irecv.at[l, s, me],
            device_id={"block": b}, device_id_type=MESH,
        )

    def reply_arrival(l, s, b):
        return pltpu.make_async_remote_copy(
            src_ref=inco.at[l, s, b], dst_ref=inc.at[l, s, b],
            send_sem=isend.at[l, s, b], recv_sem=irecv.at[l, s, b],
            device_id={"block": b}, device_id_type=MESH,
        )

    def rows_at(which):
        return pl.ds(pl.multiple_of(which * rows, rows), rows)

    def part_copy(l, s):
        return pltpu.make_async_remote_copy(
            src_ref=part.at[l, s, rows_at(other), :], dst_ref=prec.at[l, s],
            send_sem=psend.at[l, s], recv_sem=precv.at[l, s],
            device_id={"section": other}, device_id_type=MESH,
        )

    def hidden_copy(l, s, which):
        return pltpu.make_async_remote_copy(
            src_ref=h.at[l + 1, s, rows_at(which), :], dst_ref=h.at[l + 1, s, rows_at(which), :],
            send_sem=xsend.at[l, s], recv_sem=xrecv.at[l, s],
            device_id={"section": other}, device_id_type=MESH,
        )

    def front(l, s):
        if s == 0:
            @pl.when(l == core)
            def _():
                loads[1].wait()
                loads[2].wait()

            @pl.when(l != core)
            def _():
                for i in range(4):
                    arrivals[i].wait_recv()

        @pl.when(l > 0)
        def _():
            hidden_copy(l - 1, s, other).wait_recv()

        x = h[l, s].astype(F32)
        mean = jnp.mean(x * x, axis=-1, keepdims=True)
        normed = (x * lax.rsqrt(mean + EPS) * pp[l, 5:6, 0:width]).astype(BF16)
        for lo in range(0, half + bc, 256):
            xs[l, s, 8 : 8 + tokens, lo : lo + 256] = dot(normed, win[l, :, lo : lo + 256])

        @pl.when(me < blocks - 1)
        def _():
            halo_copy(l, s, me + 1).start()

        z = mine(dot(normed, rt[l])) + mine(pp[l, 7:8, 0 : 2 * heads])
        e = jnp.exp(-jnp.abs(z))
        small = e * (1.0 - e * (0.5 - e * (1.0 / 3.0 - e * 0.25)))
        step = jnp.maximum(z, 0.0) + jnp.where(e < 0.01, small, jnp.log(1.0 + e))
        ld = -step * (jnp.exp(mine(pp[l, 8:9, 0 : 2 * heads])) * LOG2E)
        hi = ld.astype(BF16)
        rest = ld - hi.astype(F32)
        mid, lo = split2(rest)
        low = tril[...]
        c = dot(low, hi) + dot(low, mid) + dot(low, lo)
        r = c - jnp.log(step) * LOG2E
        cum[s, :, 0:heads] = c
        padded = jnp.concatenate([r, jnp.zeros((tokens, 128 - heads), F32)], axis=1)
        rowt[s] = padded.T[0:heads]
        tail = jnp.exp2(c[tokens - 1 : tokens] - r)
        thi, tlo = split2(tail)
        total[s] = dot(thi, expand[...]) + dot(tlo, expand[...])

    def middle(l, s):
        @pl.when(me > 0)
        def _():
            halo_copy(l, s, me - 1).wait_recv()
            xs[l, s, 0:8, :] = halo[l, s]

        @pl.when(me == 0)
        def _():
            xs[l, s, 0:8, :] = jnp.zeros((8, half + bc), F32)

        ones = jnp.zeros((tokens, 128), F32)
        b_f32 = None
        for j in list(range(half // 128, (half + bc) // 128)) + list(range(half // 128)):
            lo = 128 * j
            if lo < half:
                col = pl.ds(pl.multiple_of(core * half + lo, 128), 128)
            else:
                col = pl.ds(inner + lo - half, 128)
            acc = pp[l, 4:5, col] + ones
            for k in range(4):
                acc = acc + xs[l, s, 5 + k : 5 + k + tokens, lo : lo + 128] * pp[l, k : k + 1, col]
            a = 0.5 * acc
            v = (a + a * jnp.tanh(a)).astype(BF16)
            act[s, :, lo : lo + 128] = v
            if lo == half:
                b_f32 = v.astype(F32)
        b = act[s, :, half : half + nstate]
        c = act[s, :, half + nstate : half + bc]
        scores[s] = dot_nt(c, b)
        bt = b_f32.T.astype(BF16)
        last = jnp.exp2(cum[s, tokens - 1 : tokens, 0:heads])
        for j in range(half // 128):
            lo = 128 * j
            weighted = (act[s, :, lo : lo + 128].astype(F32) * total[s, :, lo : lo + 128]).astype(BF16)
            state = dot(bt, weighted).T.astype(BF16)
            for q in range(2):
                hd = 2 * j + q
                msg[l, s, hd, 0:head, :] = state[head * q : head * (q + 1), :]
                d = jnp.broadcast_to(last[:, hd : hd + 1], (8, 128))
                dhi = d.astype(BF16).astype(F32)
                msg[l, s, hd, head : head + DECAY_ROWS, :] = jnp.concatenate([dhi, d - dhi], axis=0).astype(BF16)

        def send(k, _):
            state_copy(l, s, k).start()
            return 0

        lax.fori_loop(1, blocks, send, 0)

    def diagonal(l, s):
        hr = tokens // 2
        mask = lax.broadcasted_iota(jnp.int32, (hr, hr), 0) >= lax.broadcasted_iota(jnp.int32, (hr, hr), 1)
        lane = lax.broadcasted_iota(jnp.int32, (tokens, 128), 1) < head
        sk = mine(pp[l, 9:10, 0 : 2 * heads])
        for j in range(half // 128):
            lo = 128 * j
            vals = act[s, :, lo : lo + 128]
            zero = jnp.zeros_like(vals)
            gain = jnp.where(
                lane[0:1], jnp.broadcast_to(sk[:, 2 * j : 2 * j + 1], (1, 128)),
                jnp.broadcast_to(sk[:, 2 * j + 1 : 2 * j + 2], (1, 128)),
            )
            top = vals[0:hr].astype(F32) * gain
            bot = vals[hr:].astype(F32) * gain
            for q in range(2):
                hd = 2 * j + q
                v = jnp.where(lane, vals, zero) if q == 0 else jnp.where(lane, zero, vals)
                ct = jnp.broadcast_to(cum[s, 0:hr, hd : hd + 1], (hr, hr))
                cb = jnp.broadcast_to(cum[s, hr:tokens, hd : hd + 1], (hr, hr))
                r0 = rowt[s, hd : hd + 1, 0:hr]
                r1 = rowt[s, hd : hd + 1, hr:tokens]
                m00 = jnp.where(mask, jnp.exp2(ct - r0) * scores[s, 0:hr, 0:hr], 0.0).astype(BF16)
                m10 = (jnp.exp2(cb - r0) * scores[s, hr:tokens, 0:hr]).astype(BF16)
                m11 = jnp.where(mask, jnp.exp2(cb - r1) * scores[s, hr:tokens, hr:tokens], 0.0).astype(BF16)
                top = top + dot(m00, v[0:hr])
                bot = bot + dot(jnp.concatenate([m10, m11], axis=1), v)
            total[s, 0:hr, lo : lo + 128] = top
            total[s, hr:tokens, lo : lo + 128] = bot

    def scan(l, s):
        rcv[l, s, me] = msg[l, s, me]

        def step(b, state):
            @pl.when(b != me)
            def _():
                state_arrival(l, s, b).wait_recv()

            inco[l, s, b] = state.astype(BF16)

            @pl.when(b != me)
            def _():
                reply_copy(l, s, b).start()

            m = rcv[l, s, b].astype(F32)
            d = m[head : head + 8] + m[head + 8 : head + 16]
            return state * jnp.concatenate([d] * (head // 8), axis=0) + m[0:head]

        lax.fori_loop(0, blocks, step, jnp.zeros((head, nstate), F32))
        inc[l, s, me] = inco[l, s, me]

    def back(l, s):
        if s == 0:
            @pl.when(l == core)
            def _():
                loads[3].wait()

            @pl.when(l != core)
            def _():
                arrivals[4].wait_recv()

        def arrive(b, _):
            @pl.when(b != me)
            def _():
                reply_arrival(l, s, b).wait_recv()

            return 0

        lax.fori_loop(0, blocks, arrive, 0)
        c = act[s, :, half + nstate : half + bc]
        ehi, elo = split2(jnp.exp2(cum[s, :, 0:heads]))
        sq = jnp.zeros((tokens, 1), F32)
        ys = []
        per = 256 // head
        for j in range(half // 256):
            lo = 256 * j
            incoming = inc[l, s, per * j : per * (j + 1)].reshape(256, nstate)
            e = dot(ehi, expand[:, lo : lo + 256]) + dot(elo, expand[:, lo : lo + 256])
            t = total[s, :, lo : lo + 256] + dot_nt(c, incoming) * e
            sq = sq + jnp.sum(t * t, axis=-1, keepdims=True)
            gain = pp[l, 6:7, pl.ds(pl.multiple_of(core * half + lo, 256), 256)]
            ys.append((t * gain).astype(BF16))
        y = jnp.concatenate(ys, axis=1)
        for lo in range(0, width, 256):
            part[l, s, :, lo : lo + 256] = dot(y, wo[l, :, lo : lo + 256])
        part[l, s, :, width : width + 128] = jnp.broadcast_to(sq, (tokens, 128))
        part_copy(l, s).start()

    def finish(l, s):
        part_copy(l, s).wait_recv()
        at = rows_at(core)
        sq = part[l, s, at, width : width + 128] + prec[l, s, :, width : width + 128]
        scale = lax.rsqrt(sq * (1.0 / inner) + EPS)
        for lo in range(0, width, 128):
            y = part[l, s, at, lo : lo + 128] + prec[l, s, :, lo : lo + 128]
            new = h[l, s, at, lo : lo + 128].astype(F32) + y * scale
            h[l + 1, s, at, lo : lo + 128] = new.astype(BF16)
        hidden_copy(l, s, core).start()

    def layer(l, _):
        front(l, 0)
        front(l, 1)
        middle(l, 0)
        middle(l, 1)
        diagonal(l, 0)
        scan(l, 0)
        diagonal(l, 1)
        scan(l, 1)
        back(l, 0)
        back(l, 1)
        finish(l, 0)
        finish(l, 1)
        return 0

    lax.fori_loop(0, 2, layer, 0)

    for s in range(seqs):
        hidden_copy(1, s, other).wait_recv()
    result = pltpu.make_async_copy(h.at[core + 1], out.at[0], out_sem)
    result.start()
    for copy in pushes:
        copy.wait_send()

    def drain(l, _):
        for s in range(seqs):
            @pl.when(me < blocks - 1)
            def _():
                halo_copy(l, s, me + 1).wait_send()

            part_copy(l, s).wait_send()
            hidden_copy(l, s, core).wait_send()

            def one(k, _):
                state_copy(l, s, k).wait_send()
                reply_copy(l, s, lax.rem(me + k, blocks)).wait_send()
                return 0

            lax.fori_loop(1, blocks, one, 0)
        return 0

    lax.fori_loop(0, 2, drain, 0)
    result.wait()


def shards(emb, wide, rate, taps, tbias, sbias, dlog, skip, ngain, igain, proj):
    blocks = lax.axis_size("block")
    seqs, tokens, width = emb.shape
    xbc = wide.shape[2]
    inner = proj.shape[1]
    half = inner // 2
    bc = xbc - inner
    heads = sbias.shape[1] // 2
    head = half // heads
    nstate = bc // 2
    assert heads == blocks and lax.axis_size("section") == 2
    vmem = pl.BlockSpec(memory_space=pltpu.VMEM)
    hbm = pl.BlockSpec(memory_space=pl.ANY)
    V, dma = pltpu.VMEM, pltpu.SemaphoreType.DMA
    return pl.pallas_call(
        functools.partial(kernel, blocks),
        out_shape=jax.ShapeDtypeStruct((1, seqs, tokens, width), BF16),
        in_specs=[hbm, hbm] + [vmem] * 8 + [hbm],
        out_specs=hbm,
        scratch_shapes=[
            V((3, seqs, tokens, width), BF16),
            V((2, width, half + bc), BF16),
            V((2, half, width), BF16),
            V((2, width, 2 * heads), BF16),
            V((2, 16, xbc), F32),
            V((tokens, tokens), BF16),
            V((heads, half), BF16),
            V((2, seqs, tokens + 8, half + bc), F32),
            V((2, seqs, 8, half + bc), F32),
            V((seqs, tokens, half + bc), BF16),
            V((seqs, tokens, tokens), F32),
            V((seqs, tokens, 128), F32),
            V((seqs, heads, tokens), F32),
            V((seqs, tokens, half), F32),
            V((2, seqs, blocks, head + DECAY_ROWS, nstate), BF16),
            V((2, seqs, blocks, head + DECAY_ROWS, nstate), BF16),
            V((2, seqs, blocks, head, nstate), BF16),
            V((2, seqs, blocks, head, nstate), BF16),
            V((2, seqs, tokens, width + 128), F32),
            V((2, seqs, tokens // 2, width + 128), F32),
            dma((4,)), dma(()), dma((5,)), dma((5,)),
            dma((2, seqs)), dma((2, seqs)),
            dma((2, seqs, blocks)), dma((2, seqs, blocks)),
            dma((2, seqs, blocks)), dma((2, seqs, blocks)),
            dma((2, seqs)), dma((2, seqs)), dma((2, seqs)), dma((2, seqs)),
        ],
        compiler_params=pltpu.CompilerParams(
            collective_id=0, has_side_effects=True, vmem_limit_bytes=52 * 1024 * 1024
        ),
    )(emb, wide, rate, taps, tbias, sbias, dlog, skip, ngain, igain, proj)


def solution(mesh):
    placed = (
        P("dp", "block", None),
        P("section", None, None),
        P("section", None, None),
        P("section", None, None),
        P("section", None),
        P("section", None),
        P("section", None),
        P("section", None),
        P("section", None),
        P("section", None),
        P("section", None, None),
    )
    return jax.shard_map(
        shards,
        mesh=mesh,
        in_specs=placed,
        out_specs=P("section", "dp", "block", None),
        check_vma=False,
    )
```

time: 479 us -> 72.2 us (0.15)
  the two profiles are of different devices: /device:TPU:249 before, /device:TPU:1 now
where the time goes in v1:
time: 72.2 us; the launch traced here: 71.8 us
  Pallas kernels  65 us (90%)
  local copies, waits for them, and re-layouts  6.79 us (9%)
    pallas_call x1, Pallas kernels, shards(): pl.pallas_call(functools.partial(kernel, blocks), out_shape=jax.ShapeDtyp...  65 us
    unnamed x16, local copies, waits for them, and re-layouts  6.79 us

profile of v1, /device:TPU:1, one launch (start us, length us, event | category | flops | bytes accessed | tf_op | source)
XLA Modules:
  0.0 71.8 jit_solution(15279178120847510303)
XLA Ops:
  0.0 1.0 %copy.12.rate = bf16[1,1024,32]{2,1,0:T(8,128)(2,1)S(1)} copy(bf16[1,1024,32]{1,2,0:T(8,128)(2,1)} %param.13) | data formatting | bytes 131072 | tf_op args[2]
  1.0 0.0 copy-start
  1.0 0.8 %copy-done = f32[1,4,2304]{2,1,0:T(4,128)S(1)} copy-done((f32[1,4,2304]{2,1,0:T(4,128)S(1)}, f32[1,4,2304]{2,1,0:T(4,128)}, u32[]{:S(2)}) %copy-start) | copy-done | bytes 36888
  1.8 0.0 copy-start.1
  1.8 0.7 copy-done.1
  2.5 0.0 copy-start.2
  2.5 0.7 copy-done.2
  3.2 0.0 copy-start.3
  3.2 0.7 copy-done.3
  3.9 0.0 copy-start.4
  3.9 0.7 copy-done.4
  4.5 0.0 copy-start.5
  4.5 0.7 copy-done.5
  5.2 0.0 copy-start.6
  5.2 0.7 copy-done.6
  5.8 65.0 %shard_map.109 = bf16[1,2,256,1024]{3,2,1,0:T(8,128)(2,1)S(1)} custom-call(bf16[2,256,1024]{2,1,0:T(8,128)(2,1)} %emb.1, bf16[1,1024,2304]{2,1,0:T(8,128)(2,1)} %wide.1, bf16[1,1024,32]{2,1,0:T(8,128)(2,1)S(1)} %copy.12.rate, f32[1,4,2304]{2,1,0:T(4,128)S(1)} %copy-done, f32[1,2304]{1,0:T(1,128)S(1)} %copy-done.1, f32[1,32]{1,0:T(1,128)S(1)} %copy-done.4, ...), custom_call_target="tpu_custom_call" | custom-call | tf_op jit(solution)/shard_map/pallas_call | solution.py:423
  70.9 1.0 %copy.14 = bf16[1,2,256,1024]{3,2,1,0:T(8,128)(2,1)} copy(bf16[1,2,256,1024]{3,2,1,0:T(8,128)(2,1)S(1)} %shard_map.109) | data formatting | bytes 2097152
Async XLA Ops:
  1.0 0.8 %copy-start = (f32[1,4,2304]{2,1,0:T(4,128)S(1)}, f32[1,4,2304]{2,1,0:T(4,128)}, u32[]{:S(2)}) copy-start(f32[1,4,2304]{2,1,0:T(4,128)} %taps.1) | copy-start | bytes 110596
  1.8 0.7 copy-start.1
  2.5 0.7 copy-start.2
  3.2 0.7 copy-start.3
  3.9 0.7 copy-start.4
  4.5 0.7 copy-start.5
  5.2 0.7 copy-start.6

commit v2 on v1

v2 whole, which is shorter than its diff:
```python
import functools

import jax
import jax.numpy as jnp
from jax import lax
from jax.experimental import pallas as pl
from jax.experimental.pallas import tpu as pltpu
from jax.sharding import PartitionSpec as P

MESH = pl.DeviceIdType.MESH
F32, BF16 = jnp.float32, jnp.bfloat16
LOG2E = 1.4426950408889634
EPS = 1e-05
DECAY_ROWS = 16


def split2(x):
    hi = x.astype(BF16)
    return hi, (x - hi.astype(F32)).astype(BF16)


def dot(a, b):
    return jnp.dot(a, b, preferred_element_type=F32)


def dot_nt(a, b):
    return lax.dot_general(a, b, (((1,), (1,)), ((), ())), preferred_element_type=F32)


def kernel(
    blocks,
    emb, wide, rate, taps, tbias, sbias, dlog, skip, ngain, igain, proj,
    out,
    h, edge, nx, win, wo, rt, tp, tb, sb, dl, sg, ng, ig, triu, expand, colc,
    xs, halo, act, scores, cum, cols16, rowt, dk, total,
    msg, rcv, inco, inc, part, prec,
    local_sem, wsend, wrecv, esend, erecv, hsend, hrecv,
    msend, mrecv, isend, irecv, psend, precv,
):
    core = lax.axis_index("section")
    me = lax.axis_index("block")
    other = 1 - core
    seqs, tokens, width = emb.shape
    half = wo.shape[1]
    bc = win.shape[2] - half
    nstate = bc // 2
    heads = msg.shape[2]
    head = half // heads
    inner = 2 * half
    edge_rows = edge.shape[1]
    cols = 256
    chunks = (half + bc) // cols
    pieces = ((0, width // 2), (width // 2, width + 128))

    barrier = pltpu.get_barrier_semaphore()
    pl.semaphore_signal(barrier, inc=1, device_id={"section": other}, device_id_type=MESH)

    def greet(k, _):
        peer = lax.rem(me + k, blocks)
        pl.semaphore_signal(barrier, inc=1, device_id={"block": peer}, device_id_type=MESH)
        return 0

    lax.fori_loop(1, blocks, greet, 0)

    def moves(which, layer):
        found = []
        for j in range(chunks):
            at = which * half + cols * j if cols * j < half else inner + cols * j - half
            found.append((wide.at[0, :, pl.ds(pl.multiple_of(at, cols), cols)], win.at[layer, :, pl.ds(cols * j, cols)]))
        found += [(rate.at[0], rt.at[layer]), (taps.at[0], tp.at[layer])]
        found += [(a, b.at[layer]) for a, b in ((tbias, tb), (sbias, sb), (dlog, dl), (skip, sg), (ngain, ng), (igain, ig))]
        found.append((proj.at[0, pl.ds(pl.multiple_of(which * half, half), half), :], wo.at[layer]))
        return found

    local = [pltpu.make_async_copy(a, b, local_sem.at[i]) for i, (a, b) in enumerate(moves(core, core))]
    count = len(local)
    embed = pltpu.make_async_copy(emb, h.at[0], local_sem.at[count])
    embed.start()
    for copy in local[chunks:-1] + local[:chunks] + local[-1:]:
        copy.start()

    def remote(i, move):
        return pltpu.make_async_remote_copy(
            src_ref=move[0], dst_ref=move[1], send_sem=wsend.at[i], recv_sem=wrecv.at[i],
            device_id={"section": other}, device_id_type=MESH,
        )

    pushes = [remote(i, m) for i, m in enumerate(moves(other, core))]
    arrivals = [remote(i, m) for i, m in enumerate(moves(core, other))]

    def edge_copy(peer):
        return pltpu.make_async_remote_copy(
            src_ref=emb.at[:, pl.ds(tokens - edge_rows, edge_rows), :], dst_ref=edge,
            send_sem=esend, recv_sem=erecv, device_id={"block": peer}, device_id_type=MESH,
        )

    pl.semaphore_wait(barrier, blocks)
    for copy in pushes[chunks:-1] + pushes[:chunks]:
        copy.start()

    @pl.when(me < blocks - 1)
    def _():
        edge_copy(me + 1).start()

    def ready(l, which):
        @pl.when(core == l)
        def _():
            for i in which:
                local[i].wait()

        @pl.when(core != l)
        def _():
            for i in which:
                arrivals[i].wait_recv()

    ri = lax.broadcasted_iota(jnp.int32, (tokens, tokens), 0)
    ci = lax.broadcasted_iota(jnp.int32, (tokens, tokens), 1)
    triu[...] = jnp.where(ri <= ci, 1.0, 0.0).astype(BF16)
    eh = lax.broadcasted_iota(jnp.int32, (heads, half), 0)
    ec = lax.broadcasted_iota(jnp.int32, (heads, half), 1)
    spread = jnp.where((ec >= eh * head) & (ec < eh * head + head), 1.0, 0.0).astype(BF16)
    expand[...] = jnp.zeros_like(expand)
    for i, lo in ((1, 0), (2, 0), (3, half), (4, half)):
        expand[heads * i : heads * (i + 1), lo : lo + half] = spread

    def mine(row):
        return jnp.where(core == 0, row[:, 0:heads], row[:, heads : 2 * heads])

    def halo_copy(s, peer):
        return pltpu.make_async_remote_copy(
            src_ref=xs.at[1, s, pl.ds(tokens, 8), :], dst_ref=halo.at[s],
            send_sem=hsend.at[s], recv_sem=hrecv.at[s],
            device_id={"block": peer}, device_id_type=MESH,
        )

    def state_copy(l, s, k):
        peer = lax.rem(me + k, blocks)
        return pltpu.make_async_remote_copy(
            src_ref=msg.at[l, s, peer], dst_ref=rcv.at[l, s, me],
            send_sem=msend.at[l, s, k], recv_sem=mrecv.at[l, s, me],
            device_id={"block": peer}, device_id_type=MESH,
        )

    def state_arrival(l, s, b):
        return pltpu.make_async_remote_copy(
            src_ref=msg.at[l, s, b], dst_ref=rcv.at[l, s, b],
            send_sem=msend.at[l, s, 0], recv_sem=mrecv.at[l, s, b],
            device_id={"block": b}, device_id_type=MESH,
        )

    def reply_copy(l, s, b):
        return pltpu.make_async_remote_copy(
            src_ref=inco.at[l, s, b], dst_ref=inc.at[l, s, me],
            send_sem=isend.at[l, s, b], recv_sem=irecv.at[l, s, me],
            device_id={"block": b}, device_id_type=MESH,
        )

    def reply_arrival(l, s, b):
        return pltpu.make_async_remote_copy(
            src_ref=inco.at[l, s, b], dst_ref=inc.at[l, s, b],
            send_sem=isend.at[l, s, b], recv_sem=irecv.at[l, s, b],
            device_id={"block": b}, device_id_type=MESH,
        )

    def part_copy(l, s, i):
        at = pl.ds(pieces[i][0], pieces[i][1] - pieces[i][0])
        return pltpu.make_async_remote_copy(
            src_ref=part.at[l, s, :, at], dst_ref=prec.at[l, s, :, at],
            send_sem=psend.at[l, s, i], recv_sem=precv.at[l, s, i],
            device_id={"section": other}, device_id_type=MESH,
        )

    def normalize(l, x):
        x = x.astype(F32)
        mean = jnp.mean(x * x, axis=-1, keepdims=True)
        return (x * lax.rsqrt(mean + EPS) * ng[l]).astype(BF16)

    def columns(l):
        ready(l, range(chunks, count - 1))
        for i, row in ((0, mine(sb[l])), (1, jnp.exp(mine(dl[l])) * LOG2E)):
            wide_row = jnp.concatenate([row, jnp.zeros((1, 128 - heads), F32)], axis=1)
            colc[l, i] = jnp.broadcast_to(wide_row, (128, 128)).T[0:heads]

    def rates(l, s, normed):
        both = dot_nt(rt[l], normed)
        z = jnp.where(core == 0, both[0:heads], both[heads : 2 * heads])
        z = z + jnp.concatenate([colc[l, 0]] * (tokens // 128), axis=1)
        e = jnp.exp(-jnp.abs(z))
        small = e * (1.0 - e * (0.5 - e * (1.0 / 3.0 - e * 0.25)))
        step = jnp.maximum(z, 0.0) + jnp.where(e < 0.01, small, jnp.log(1.0 + e))
        ld = -step * jnp.concatenate([colc[l, 1]] * (tokens // 128), axis=1)
        hi = ld.astype(BF16)
        mid, lo = split2(ld - hi.astype(F32))
        c3 = dot(jnp.concatenate([hi, mid, lo], axis=0), triu[...])
        c = c3[0:heads] + c3[heads : 2 * heads] + c3[2 * heads : 3 * heads]
        r = c - jnp.log(step) * LOG2E
        rowt[s] = r
        last = jnp.broadcast_to(c[:, tokens - 1 : tokens], (heads, tokens))
        tail = jnp.exp2(last - r)
        thi = tail.astype(BF16).astype(F32)
        grown = jnp.exp2(c)
        ghi = grown.astype(BF16).astype(F32)
        stack = [c, thi, tail - thi, ghi, grown - ghi, jnp.zeros((128 - 5 * heads, tokens), F32)]
        col = jnp.concatenate(stack, axis=0).T
        cum[s] = col
        narrow = col.astype(BF16)
        cols16[s] = narrow
        total[s] = dot(narrow, expand[:, 0:half])
        d = jnp.exp2(last[:, 0:128])
        dhi = d.astype(BF16).astype(F32)
        dk[s, 0:heads] = dhi
        dk[s, heads : 2 * heads] = d - dhi

    def front_both():
        embed.wait()
        columns(0)
        span = edge_rows + tokens
        for s in range(seqs):
            normed = normalize(0, h[0, s])
            nx[span * s + edge_rows : span * (s + 1)] = normed
            rates(0, s, normed)

        @pl.when(me > 0)
        def _():
            edge_copy(me).wait_recv()

        @pl.when(me == 0)
        def _():
            edge[...] = jnp.zeros_like(edge)

        for s in range(seqs):
            nx[span * s : span * s + edge_rows] = normalize(0, edge[s])
        for j in range(chunks):
            ready(0, [j])
            made = dot(nx[...], win[0, :, cols * j : cols * (j + 1)])
            for s in range(seqs):
                xs[0, s, :, cols * j : cols * (j + 1)] = made[span * (s + 1) - tokens - 8 : span * (s + 1)]

    def front(s):
        normed = normalize(1, h[1, s])
        for lo in range(0, half + bc, cols):
            xs[1, s, 8 : 8 + tokens, lo : lo + cols] = dot(normed, win[1, :, lo : lo + cols])

        @pl.when(me < blocks - 1)
        def _():
            halo_copy(s, me + 1).start()

        rates(1, s, normed)

    def middle(l, s):
        if l == 1:
            @pl.when(me > 0)
            def _():
                halo_copy(s, me).wait_recv()
                xs[1, s, 0:8, :] = halo[s]

            @pl.when(me == 0)
            def _():
                xs[1, s, 0:8, :] = jnp.zeros((8, half + bc), F32)

        b_f32 = None
        for j in list(range(half // 128, (half + bc) // 128)) + list(range(half // 128)):
            lo = 128 * j
            if lo < half:
                col = pl.ds(pl.multiple_of(core * half + lo, 128), 128)
            else:
                col = pl.ds(inner + lo - half, 128)
            acc = tb[l, :, col] + xs[l, s, 8 : 8 + tokens, lo : lo + 128] * tp[l, 3:4, col]
            for k in range(3):
                acc = acc + xs[l, s, 5 + k : 5 + k + tokens, lo : lo + 128] * tp[l, k : k + 1, col]
            a = 0.5 * acc
            v = (a + a * jnp.tanh(a)).astype(BF16)
            act[s, :, lo : lo + 128] = v
            if lo == half:
                b_f32 = v.astype(F32)
        bt = b_f32.T.astype(BF16)
        for j in range(half // 128):
            lo = 128 * j
            weighted = (act[s, :, lo : lo + 128].astype(F32) * total[s, :, lo : lo + 128]).astype(BF16)
            state = dot(bt, weighted).T.astype(BF16)
            for q in range(2):
                hd = 2 * j + q
                msg[l, s, hd, 0:head, :] = state[head * q : head * (q + 1), :]
                both = [jnp.broadcast_to(dk[s, i : i + 1, :], (8, 128)) for i in (hd, heads + hd)]
                msg[l, s, hd, head : head + DECAY_ROWS, :] = jnp.concatenate(both, axis=0).astype(BF16)

        def send(k, _):
            state_copy(l, s, k).start()
            return 0

        lax.fori_loop(1, blocks, send, 0)

    def diagonal(l, s):
        hr = tokens // 2
        b = act[s, :, half : half + nstate]
        c = act[s, :, half + nstate : half + bc]
        scores[...] = dot_nt(c, b)
        mask = lax.broadcasted_iota(jnp.int32, (hr, hr), 0) >= lax.broadcasted_iota(jnp.int32, (hr, hr), 1)
        lane = lax.broadcasted_iota(jnp.int32, (tokens, 128), 1) < head
        sk = mine(sg[l])
        for j in range(half // 128):
            lo = 128 * j
            vals = act[s, :, lo : lo + 128]
            zero = jnp.zeros_like(vals)
            gain = jnp.where(
                lane[0:1], jnp.broadcast_to(sk[:, 2 * j : 2 * j + 1], (1, 128)),
                jnp.broadcast_to(sk[:, 2 * j + 1 : 2 * j + 2], (1, 128)),
            )
            top = vals[0:hr].astype(F32) * gain
            bot = vals[hr:].astype(F32) * gain
            for q in range(2):
                hd = 2 * j + q
                v = jnp.where(lane, vals, zero) if q == 0 else jnp.where(lane, zero, vals)
                ct = jnp.broadcast_to(cum[s, 0:hr, hd : hd + 1], (hr, hr))
                cb = jnp.broadcast_to(cum[s, hr:tokens, hd : hd + 1], (hr, hr))
                r0 = rowt[s, hd : hd + 1, 0:hr]
                r1 = rowt[s, hd : hd + 1, hr:tokens]
                m00 = jnp.where(mask, jnp.exp2(ct - r0) * scores[0:hr, 0:hr], 0.0).astype(BF16)
                m10 = (jnp.exp2(cb - r0) * scores[hr:tokens, 0:hr]).astype(BF16)
                m11 = jnp.where(mask, jnp.exp2(cb - r1) * scores[hr:tokens, hr:tokens], 0.0).astype(BF16)
                top = top + dot(m00, v[0:hr])
                bot = bot + dot(jnp.concatenate([m10, m11], axis=1), v)
            total[s, 0:hr, lo : lo + 128] = top
            total[s, hr:tokens, lo : lo + 128] = bot

    def scan(l, s):
        rcv[l, s, me] = msg[l, s, me]

        def step(b, state):
            @pl.when(b != me)
            def _():
                state_arrival(l, s, b).wait_recv()

            inco[l, s, b] = state.astype(BF16)

            @pl.when(b != me)
            def _():
                reply_copy(l, s, b).start()

            m = rcv[l, s, b].astype(F32)
            d = m[head : head + 8] + m[head + 8 : head + 16]
            return state * jnp.concatenate([d] * (head // 8), axis=0) + m[0:head]

        lax.fori_loop(0, blocks, step, jnp.zeros((head, nstate), F32))
        inc[l, s, me] = inco[l, s, me]

    def back(l, s):
        if s == 0:
            ready(l, [count - 1])

        def arrive(b, _):
            @pl.when(b != me)
            def _():
                reply_arrival(l, s, b).wait_recv()

            return 0

        c = act[s, :, half + nstate : half + bc]
        grown = cols16[s]
        sq = jnp.zeros((tokens, 1), F32)
        ys = []
        per = 256 // head
        for j in range(half // 256):
            lo = 256 * j
            lax.fori_loop(per * j, per * (j + 1), arrive, 0)
            incoming = inc[l, s, per * j : per * (j + 1)].reshape(256, nstate)
            e = dot(grown, expand[:, half + lo : half + lo + 256])
            t = total[s, :, lo : lo + 256] + dot_nt(c, incoming) * e
            sq = sq + jnp.sum(t * t, axis=-1, keepdims=True)
            gain = ig[l, :, pl.ds(pl.multiple_of(core * half + lo, 256), 256)]
            ys.append((t * gain).astype(BF16))
        y = jnp.concatenate(ys, axis=1)
        shi = sq.astype(BF16).astype(F32)
        first = lax.broadcasted_iota(jnp.int32, (tokens, 128), 1) < 64
        part[l, s, :, width : width + 128] = jnp.where(first, shi, sq - shi).astype(BF16)
        for i in range(2):
            for lo in range(width // 2 * i, width // 2 * (i + 1), cols):
                part[l, s, :, lo : lo + cols] = dot(y, wo[l, :, lo : lo + cols]).astype(BF16)
            if l == 0:
                part_copy(l, s, i).start()
            else:
                pl.when(core == 0)(part_copy(l, s, i).start)

    def finish(l, s, store):
        for i in range(2):
            part_copy(l, s, i).wait_recv()
        sq = 0.0
        for lo in (width, width + 64):
            sq = sq + part[l, s, :, lo : lo + 1].astype(F32) + prec[l, s, :, lo : lo + 1].astype(F32)
        scale = jnp.broadcast_to(lax.rsqrt(sq * (1.0 / inner) + EPS), (tokens, 128))
        for lo in range(0, width, 128):
            y = part[l, s, :, lo : lo + 128].astype(F32) + prec[l, s, :, lo : lo + 128].astype(F32)
            new = h[l, s, :, lo : lo + 128].astype(F32) + y * scale
            store(lo, new.astype(BF16))

    def hidden_store(s):
        def store(lo, new):
            h[1, s, :, lo : lo + 128] = new

        return store

    def result_store(s):
        def store(lo, new):
            out[0, s, :, lo : lo + 128] = new

        return store

    def exchange(l):
        middle(l, 0)
        middle(l, 1)
        if l == 0:
            pushes[-1].start()
            columns(1)
        else:
            @pl.when(core == 0)
            def _():
                out[0] = h[1]
        diagonal(l, 0)
        scan(l, 0)
        diagonal(l, 1)
        scan(l, 1)
        back(l, 0)
        back(l, 1)

    front_both()
    exchange(0)
    ready(1, range(chunks))
    for s in range(seqs):
        finish(0, s, hidden_store(s))
        front(s)
    exchange(1)
    for s in range(seqs):
        pl.when(core == 1)(functools.partial(finish, 1, s, result_store(s)))

    for copy in pushes:
        copy.wait_send()

    @pl.when(me < blocks - 1)
    def _():
        edge_copy(me + 1).wait_send()
        for s in range(seqs):
            halo_copy(s, me + 1).wait_send()

    for s in range(seqs):
        for i in range(2):
            part_copy(0, s, i).wait_send()
            pl.when(core == 0)(part_copy(1, s, i).wait_send)

    def drain(k, _):
        for l in range(2):
            for s in range(seqs):
                state_copy(l, s, k).wait_send()
                reply_copy(l, s, lax.rem(me + k, blocks)).wait_send()
        return 0

    lax.fori_loop(1, blocks, drain, 0)


def shards(emb, wide, rate, taps, tbias, sbias, dlog, skip, ngain, igain, proj):
    blocks = lax.axis_size("block")
    seqs, tokens, width = emb.shape
    xbc = wide.shape[2]
    inner = proj.shape[1]
    half = inner // 2
    bc = xbc - inner
    heads = sbias.shape[1] // 2
    head = half // heads
    nstate = bc // 2
    assert heads == blocks and lax.axis_size("section") == 2
    hbm = pl.BlockSpec(memory_space=pltpu.HBM)
    V, dma = pltpu.VMEM, pltpu.SemaphoreType.DMA
    moved = (half + bc) // 256 + 9
    return pl.pallas_call(
        functools.partial(kernel, blocks),
        out_shape=jax.ShapeDtypeStruct((1, seqs, tokens, width), BF16),
        in_specs=[hbm] * 11,
        out_specs=pl.BlockSpec(memory_space=pltpu.VMEM),
        scratch_shapes=[
            V((2, seqs, tokens, width), BF16),
            V((seqs, 16, width), BF16),
            V((seqs * (tokens + 16), width), BF16),
            V((2, width, half + bc), BF16),
            V((2, half, width), BF16),
            V((2, 2 * heads, width), BF16),
            V((2, 4, xbc), F32),
            V((2, 1, xbc), F32),
            V((2, 1, 2 * heads), F32),
            V((2, 1, 2 * heads), F32),
            V((2, 1, 2 * heads), F32),
            V((2, 1, width), F32),
            V((2, 1, inner), F32),
            V((tokens, tokens), BF16),
            V((128, 2 * half), BF16),
            V((2, 2, heads, 128), F32),
            V((2, seqs, tokens + 8, half + bc), F32),
            V((seqs, 8, half + bc), F32),
            V((seqs, tokens, half + bc), BF16),
            V((tokens, tokens), F32),
            V((seqs, tokens, 128), F32),
            V((seqs, tokens, 128), BF16),
            V((seqs, heads, tokens), F32),
            V((seqs, 2 * heads, 128), F32),
            V((seqs, tokens, half), F32),
            V((2, seqs, blocks, head + DECAY_ROWS, nstate), BF16),
            V((2, seqs, blocks, head + DECAY_ROWS, nstate), BF16),
            V((2, seqs, blocks, head, nstate), BF16),
            V((2, seqs, blocks, head, nstate), BF16),
            V((2, seqs, tokens, width + 128), BF16),
            V((2, seqs, tokens, width + 128), BF16),
            dma((moved + 1,)), dma((moved,)), dma((moved,)), dma(()), dma(()),
            dma((seqs,)), dma((seqs,)),
            dma((2, seqs, blocks)), dma((2, seqs, blocks)),
            dma((2, seqs, blocks)), dma((2, seqs, blocks)),
            dma((2, seqs, 2)), dma((2, seqs, 2)),
        ],
        compiler_params=pltpu.CompilerParams(
            collective_id=0, has_side_effects=True, vmem_limit_bytes=63 * 1024 * 1024
        ),
    )(emb, wide, jnp.swapaxes(rate, 1, 2), taps, tbias, sbias, dlog, skip, ngain, igain, proj)


def solution(mesh):
    placed = (
        P("dp", "block", None),
        P("section", None, None),
        P("section", None, None),
        P("section", None, None),
        P("section", None),
        P("section", None),
        P("section", None),
        P("section", None),
        P("section", None),
        P("section", None),
        P("section", None, None),
    )
    return jax.shard_map(
        shards,
        mesh=mesh,
        in_specs=placed,
        out_specs=P("section", "dp", "block", None),
        check_vma=False,
    )
```

time: 72.2 us -> 66.9 us (0.927)
  the two profiles are of different devices: /device:TPU:1 before, /device:TPU:249 now
where the time goes in v2:
time: 66.9 us; the launch traced here: 65.8 us
  Pallas kernels  63.5 us (95%)
  local copies, waits for them, and re-layouts  2.26 us (3%)
    pallas_call x1, Pallas kernels, shards(): pl.pallas_call(functools.partial(kernel, blocks), out_shape=jax.ShapeDtyp...  63.5 us
    unnamed x1, local copies, waits for them, and re-layouts  2.26 us

profile of v2, /device:TPU:249, one launch (start us, length us, event | category | flops | bytes accessed | tf_op | source)
XLA Modules:
  0.0 65.8 jit_solution(15621364717967075744)
XLA Ops:
  0.0 63.5 %shard_map.109 = bf16[1,2,256,1024]{3,2,1,0:T(8,128)(2,1)} custom-call(bf16[2,256,1024]{2,1,0:T(8,128)(2,1)} %emb.1, bf16[1,1024,2304]{2,1,0:T(8,128)(2,1)} %wide.1, bf16[1,32,1024]{2,1,0:T(8,128)(2,1)} %bitcast.1, f32[1,4,2304]{2,1,0:T(4,128)} %taps.1, f32[1,2304]{1,0:T(1,128)} %tbias.1, f32[1,32]{1,0:T(1,128)} %sbias.1, f32[1,32]{1,0:T(1,128)} %dlog.1, ...), custom_call_target="tpu_custom_call" | custom-call | tf_op jit(solution)/shard_map/pallas_call | solution.py:473
  63.5 2.3 %copy.13 = bf16[1,2,256,1024]{3,2,1,0:T(8,128)(2,1)} copy(bf16[1,2,256,1024]{3,2,1,0:T(8,128)(2,1)} %shard_map.109) | data formatting | bytes 2097152

commit v3 on v2

--- a/solution.py
+++ b/solution.py
@@ -31,7 +31,7 @@
     blocks,
     emb, wide, rate, taps, tbias, sbias, dlog, skip, ngain, igain, proj,
     out,
-    h, edge, nx, win, wo, rt, tp, tb, sb, dl, sg, ng, ig, triu, expand, colc,
+    h, edge, nx, win, wo, rt, rk, tp, tb, sb, dl, sg, ng, ig, triu, expand, colc,
     xs, halo, act, scores, cum, cols16, rowt, dk, total,
     msg, rcv, inco, inc, part, prec,
     local_sem, wsend, wrecv, esend, erecv, hsend, hrecv,
@@ -50,7 +50,7 @@
     edge_rows = edge.shape[1]
     cols = 256
     chunks = (half + bc) // cols
-    pieces = ((0, width // 2), (width // 2, width + 128))
+    pieces = [(0 if lo == 0 else lo + 128, lo + 128 + cols) for lo in range(0, width, cols)]
 
     barrier = pltpu.get_barrier_semaphore()
     pl.semaphore_signal(barrier, inc=1, device_id={"section": other}, device_id_type=MESH)
@@ -133,18 +133,17 @@
             device_id={"block": peer}, device_id_type=MESH,
         )
 
-    def state_copy(l, s, k):
-        peer = lax.rem(me + k, blocks)
-        return pltpu.make_async_remote_copy(
-            src_ref=msg.at[l, s, peer], dst_ref=rcv.at[l, s, me],
-            send_sem=msend.at[l, s, k], recv_sem=mrecv.at[l, s, me],
-            device_id={"block": peer}, device_id_type=MESH,
+    def state_copy(l, s, b):
+        return pltpu.make_async_remote_copy(
+            src_ref=msg.at[l, s, b], dst_ref=rcv.at[l, s, me],
+            send_sem=msend.at[l, s, b], recv_sem=mrecv.at[l, s, me],
+            device_id={"block": b}, device_id_type=MESH,
         )
 
     def state_arrival(l, s, b):
         return pltpu.make_async_remote_copy(
             src_ref=msg.at[l, s, b], dst_ref=rcv.at[l, s, b],
-            send_sem=msend.at[l, s, 0], recv_sem=mrecv.at[l, s, b],
+            send_sem=msend.at[l, s, b], recv_sem=mrecv.at[l, s, b],
             device_id={"block": b}, device_id_type=MESH,
         )
 
@@ -180,9 +179,11 @@
         for i, row in ((0, mine(sb[l])), (1, jnp.exp(mine(dl[l])) * LOG2E)):
             wide_row = jnp.concatenate([row, jnp.zeros((1, 128 - heads), F32)], axis=1)
             colc[l, i] = jnp.broadcast_to(wide_row, (128, 128)).T[0:heads]
+        tall = jnp.concatenate([rt[l].astype(F32), jnp.zeros((128 - 2 * heads, width), F32)], axis=0)
+        rk[l] = tall.T.astype(BF16)
 
     def rates(l, s, normed):
-        both = dot_nt(rt[l], normed)
+        both = dot(normed, rk[l]).T
         z = jnp.where(core == 0, both[0:heads], both[heads : 2 * heads])
         z = z + jnp.concatenate([colc[l, 0]] * (tokens // 128), axis=1)
         e = jnp.exp(-jnp.abs(z))
@@ -205,7 +206,6 @@
         cum[s] = col
         narrow = col.astype(BF16)
         cols16[s] = narrow
-        total[s] = dot(narrow, expand[:, 0:half])
         d = jnp.exp2(last[:, 0:128])
         dhi = d.astype(BF16).astype(F32)
         dk[s, 0:heads] = dhi
@@ -247,6 +247,19 @@
 
         rates(1, s, normed)
 
+    def convolved(l, s, lo):
+        if lo < half:
+            col = pl.ds(pl.multiple_of(core * half + lo, 128), 128)
+        else:
+            col = pl.ds(inner + lo - half, 128)
+        acc = tb[l, :, col] + xs[l, s, 8 : 8 + tokens, lo : lo + 128] * tp[l, 3:4, col]
+        for k in range(3):
+            acc = acc + xs[l, s, 5 + k : 5 + k + tokens, lo : lo + 128] * tp[l, k : k + 1, col]
+        a = 0.5 * acc
+        v = (a + a * jnp.tanh(a)).astype(BF16)
+        act[s, :, lo : lo + 128] = v
+        return v
+
     def middle(l, s):
         if l == 1:
             @pl.when(me > 0)
@@ -258,42 +271,32 @@
             def _():
                 xs[1, s, 0:8, :] = jnp.zeros((8, half + bc), F32)
 
-        b_f32 = None
-        for j in list(range(half // 128, (half + bc) // 128)) + list(range(half // 128)):
-            lo = 128 * j
-            if lo < half:
-                col = pl.ds(pl.multiple_of(core * half + lo, 128), 128)
-            else:
-                col = pl.ds(inner + lo - half, 128)
-            acc = tb[l, :, col] + xs[l, s, 8 : 8 + tokens, lo : lo + 128] * tp[l, 3:4, col]
-            for k in range(3):
-                acc = acc + xs[l, s, 5 + k : 5 + k + tokens, lo : lo + 128] * tp[l, k : k + 1, col]
-            a = 0.5 * acc
-            v = (a + a * jnp.tanh(a)).astype(BF16)
-            act[s, :, lo : lo + 128] = v
-            if lo == half:
-                b_f32 = v.astype(F32)
-        bt = b_f32.T.astype(BF16)
-        for j in range(half // 128):
-            lo = 128 * j
-            weighted = (act[s, :, lo : lo + 128].astype(F32) * total[s, :, lo : lo + 128]).astype(BF16)
+        bt = convolved(l, s, half).astype(F32).T.astype(BF16)
+        per = 256 // head
+        for j in range(half // 256):
+            lo = 256 * j
+            v = jnp.concatenate([convolved(l, s, lo), convolved(l, s, lo + 128)], axis=1)
+            weighted = (v.astype(F32) * dot(cols16[s], expand[:, lo : lo + 256])).astype(BF16)
             state = dot(bt, weighted).T.astype(BF16)
-            for q in range(2):
-                hd = 2 * j + q
+            for q in range(per):
+                hd = per * j + q
                 msg[l, s, hd, 0:head, :] = state[head * q : head * (q + 1), :]
                 both = [jnp.broadcast_to(dk[s, i : i + 1, :], (8, 128)) for i in (hd, heads + hd)]
                 msg[l, s, hd, head : head + DECAY_ROWS, :] = jnp.concatenate(both, axis=0).astype(BF16)
 
-        def send(k, _):
-            state_copy(l, s, k).start()
-            return 0
-
-        lax.fori_loop(1, blocks, send, 0)
+            def send(b, _):
+                @pl.when(b != me)
+                def _():
+                    state_copy(l, s, b).start()
+
+                return 0
+
+            lax.fori_loop(per * j, per * (j + 1), send, 0)
 
     def diagonal(l, s):
         hr = tokens // 2
         b = act[s, :, half : half + nstate]
-        c = act[s, :, half + nstate : half + bc]
+        c = convolved(l, s, half + nstate)
         scores[...] = dot_nt(c, b)
         mask = lax.broadcasted_iota(jnp.int32, (hr, hr), 0) >= lax.broadcasted_iota(jnp.int32, (hr, hr), 1)
         lane = lax.broadcasted_iota(jnp.int32, (tokens, 128), 1) < head
@@ -345,9 +348,6 @@
         inc[l, s, me] = inco[l, s, me]
 
     def back(l, s):
-        if s == 0:
-            ready(l, [count - 1])
-
         def arrive(b, _):
             @pl.when(b != me)
             def _():
@@ -372,26 +372,27 @@
         y = jnp.concatenate(ys, axis=1)
         shi = sq.astype(BF16).astype(F32)
         first = lax.broadcasted_iota(jnp.int32, (tokens, 128), 1) < 64
-        part[l, s, :, width : width + 128] = jnp.where(first, shi, sq - shi).astype(BF16)
-        for i in range(2):
-            for lo in range(width // 2 * i, width // 2 * (i + 1), cols):
-                part[l, s, :, lo : lo + cols] = dot(y, wo[l, :, lo : lo + cols]).astype(BF16)
+        part[l, s, :, 0:128] = jnp.where(first, shi, sq - shi).astype(BF16)
+        for i, lo in enumerate(range(0, width, cols)):
+            part[l, s, :, 128 + lo : 128 + lo + cols] = dot(y, wo[l, :, lo : lo + cols]).astype(BF16)
             if l == 0:
                 part_copy(l, s, i).start()
             else:
                 pl.when(core == 0)(part_copy(l, s, i).start)
 
     def finish(l, s, store):
-        for i in range(2):
+        for i in range(width // cols):
             part_copy(l, s, i).wait_recv()
-        sq = 0.0
-        for lo in (width, width + 64):
-            sq = sq + part[l, s, :, lo : lo + 1].astype(F32) + prec[l, s, :, lo : lo + 1].astype(F32)
-        scale = jnp.broadcast_to(lax.rsqrt(sq * (1.0 / inner) + EPS), (tokens, 128))
-        for lo in range(0, width, 128):
-            y = part[l, s, :, lo : lo + 128].astype(F32) + prec[l, s, :, lo : lo + 128].astype(F32)
-            new = h[l, s, :, lo : lo + 128].astype(F32) + y * scale
-            store(lo, new.astype(BF16))
+            if i == 0:
+                sq = 0.0
+                for at in (0, 64):
+                    sq = sq + part[l, s, :, at : at + 1].astype(F32) + prec[l, s, :, at : at + 1].astype(F32)
+                scale = jnp.broadcast_to(lax.rsqrt(sq * (1.0 / inner) + EPS), (tokens, 128))
+            for lo in range(cols * i, cols * (i + 1), 128):
+                at = slice(128 + lo, 256 + lo)
+                y = part[l, s, :, at].astype(F32) + prec[l, s, :, at].astype(F32)
+                new = h[l, s, :, lo : lo + 128].astype(F32) + y * scale
+                store(lo, new.astype(BF16))
 
     def hidden_store(s):
         def store(lo, new):
@@ -405,9 +406,15 @@
 
         return store
 
+    def each(run):
+        def body(s, _):
+            run(s)
+            return 0
+
+        lax.fori_loop(0, seqs, body, 0)
+
     def exchange(l):
-        middle(l, 0)
-        middle(l, 1)
+        each(lambda s: middle(l, s))
         if l == 0:
             pushes[-1].start()
             columns(1)
@@ -415,22 +422,19 @@
             @pl.when(core == 0)
             def _():
                 out[0] = h[1]
-        diagonal(l, 0)
-        scan(l, 0)
-        diagonal(l, 1)
-        scan(l, 1)
-        back(l, 0)
-        back(l, 1)
+        each(lambda s: (diagonal(l, s), scan(l, s)))
+        ready(l, [count - 1])
+        each(lambda s: back(l, s))
 
     front_both()
     exchange(0)
     ready(1, range(chunks))
-    for s in range(seqs):
-        finish(0, s, hidden_store(s))
-        front(s)
+    each(lambda s: (finish(0, s, hidden_store(s)), front(s)))
     exchange(1)
-    for s in range(seqs):
-        pl.when(core == 1)(functools.partial(finish, 1, s, result_store(s)))
+
+    @pl.when(core == 1)
+    def _():
+        each(lambda s: finish(1, s, result_store(s)))
 
     for copy in pushes:
         copy.wait_send()
@@ -442,15 +446,16 @@
             halo_copy(s, me + 1).wait_send()
 
     for s in range(seqs):
-        for i in range(2):
+        for i in range(width // cols):
             part_copy(0, s, i).wait_send()
             pl.when(core == 0)(part_copy(1, s, i).wait_send)
 
     def drain(k, _):
         for l in range(2):
             for s in range(seqs):
-                state_copy(l, s, k).wait_send()
-                reply_copy(l, s, lax.rem(me + k, blocks)).wait_send()
+                peer = lax.rem(me + k, blocks)
+                state_copy(l, s, peer).wait_send()
+                reply_copy(l, s, peer).wait_send()
         return 0
 
     lax.fori_loop(1, blocks, drain, 0)
@@ -468,6 +473,8 @@
     nstate = bc // 2
     assert heads == blocks and lax.axis_size("section") == 2
     hbm = pl.BlockSpec(memory_space=pltpu.HBM)
+    operands = (emb, wide, jnp.swapaxes(rate, 1, 2), taps, tbias, sbias, dlog, skip, ngain, igain, proj)
+    operands = [pltpu.with_memory_space_constraint(x, pltpu.HBM) for x in operands]
     V, dma = pltpu.VMEM, pltpu.SemaphoreType.DMA
     moved = (half + bc) // 256 + 9
     return pl.pallas_call(
@@ -482,6 +489,7 @@
             V((2, width, half + bc), BF16),
             V((2, half, width), BF16),
             V((2, 2 * heads, width), BF16),
+            V((2, width, 128), BF16),
             V((2, 4, xbc), F32),
             V((2, 1, xbc), F32),
             V((2, 1, 2 * heads), F32),
@@ -511,12 +519,12 @@
             dma((seqs,)), dma((seqs,)),
             dma((2, seqs, blocks)), dma((2, seqs, blocks)),
             dma((2, seqs, blocks)), dma((2, seqs, blocks)),
-            dma((2, seqs, 2)), dma((2, seqs, 2)),
+            dma((2, seqs, width // 256)), dma((2, seqs, width // 256)),
         ],
         compiler_params=pltpu.CompilerParams(
-            collective_id=0, has_side_effects=True, vmem_limit_bytes=63 * 1024 * 1024
+            collective_id=0, has_side_effects=True, vmem_limit_bytes=52 * 1024 * 1024
         ),
-    )(emb, wide, jnp.swapaxes(rate, 1, 2), taps, tbias, sbias, dlog, skip, ngain, igain, proj)
+    )(*operands)
 
 
 def solution(mesh):

time: 66.9 us -> 64.1 us (0.958)
  local copies, waits for them, and re-layouts: 2.26 us -> 0.97 us
  Pallas kernels: 63.5 us -> 62.5 us
    unnamed x1, local copies, waits for them, and re-layouts: 2.26 us -> 0.97 us
    pallas_call x1, Pallas kernels: 63.5 us -> 62.5 us  [shards(): pl.pallas_call(functools.partial(kernel, blocks), out_shape=jax.ShapeDtyp...]
where the time goes in v3:
time: 64.1 us; the launch traced here: 63.5 us
  Pallas kernels  62.5 us (98%)
  local copies, waits for them, and re-layouts  0.97 us (2%)
    pallas_call x1, Pallas kernels, shards(): pl.pallas_call(functools.partial(kernel, blocks), out_shape=jax.ShapeDtyp...  62.5 us

profile of v3, /device:TPU:249, one launch (start us, length us, event | category | flops | bytes accessed | tf_op | source)
XLA Modules:
  0.0 63.5 jit_solution(1829772487525493286)
XLA Ops:
  0.0 62.5 %shard_map.109 = bf16[1,2,256,1024]{3,2,1,0:T(8,128)(2,1)S(1)} custom-call(bf16[2,256,1024]{2,1,0:T(8,128)(2,1)} %emb.1, bf16[1,1024,2304]{2,1,0:T(8,128)(2,1)} %wide.1, bf16[1,32,1024]{2,1,0:T(8,128)(2,1)} %bitcast.1, f32[1,4,2304]{2,1,0:T(4,128)} %taps.1, f32[1,2304]{1,0:T(1,128)} %tbias.1, f32[1,32]{1,0:T(1,128)} %sbias.1, f32[1,32]{1,0:T(1,128)} %dlog.1, ...), custom_call_target="tpu_custom_call" | custom-call | tf_op jit(solution)/shard_map/pallas_call | solution.py:480
  62.5 1.0 %copy.13 = bf16[1,2,256,1024]{3,2,1,0:T(8,128)(2,1)} copy(bf16[1,2,256,1024]{3,2,1,0:T(8,128)(2,1)S(1)} %shard_map.109) | data formatting | bytes 2097152

commit v4 on v3

--- a/solution.py
+++ b/solution.py
@@ -122,6 +122,10 @@
     expand[...] = jnp.zeros_like(expand)
     for i, lo in ((1, 0), (2, 0), (3, half), (4, half)):
         expand[heads * i : heads * (i + 1), lo : lo + half] = spread
+
+    @pl.when(me == 0)
+    def _():
+        inc[...] = jnp.zeros_like(inc)
 
     def mine(row):
         return jnp.where(core == 0, row[:, 0:heads], row[:, heads : 2 * heads])
@@ -281,11 +285,11 @@
             for q in range(per):
                 hd = per * j + q
                 msg[l, s, hd, 0:head, :] = state[head * q : head * (q + 1), :]
-                both = [jnp.broadcast_to(dk[s, i : i + 1, :], (8, 128)) for i in (hd, heads + hd)]
+                both = [jnp.broadcast_to(dk[s, i : i + 1, :], (DECAY_ROWS // 2, 128)) for i in (hd, heads + hd)]
                 msg[l, s, hd, head : head + DECAY_ROWS, :] = jnp.concatenate(both, axis=0).astype(BF16)
 
             def send(b, _):
-                @pl.when(b != me)
+                @pl.when((b != me) & (me < blocks - 1))
                 def _():
                     state_copy(l, s, b).start()
 
@@ -329,27 +333,31 @@
     def scan(l, s):
         rcv[l, s, me] = msg[l, s, me]
 
+        def reply(b, state):
+            inco[l, s, b] = state.astype(BF16)
+
+            @pl.when((b != me) & (b > 0))
+            def _():
+                reply_copy(l, s, b).start()
+
         def step(b, state):
+            reply(b, state)
+
             @pl.when(b != me)
             def _():
                 state_arrival(l, s, b).wait_recv()
 
-            inco[l, s, b] = state.astype(BF16)
-
-            @pl.when(b != me)
-            def _():
-                reply_copy(l, s, b).start()
-
             m = rcv[l, s, b].astype(F32)
-            d = m[head : head + 8] + m[head + 8 : head + 16]
-            return state * jnp.concatenate([d] * (head // 8), axis=0) + m[0:head]
-
-        lax.fori_loop(0, blocks, step, jnp.zeros((head, nstate), F32))
+            at = [head, head + DECAY_ROWS // 2]
+            d = m[at[0] : at[0] + 1] + m[at[1] : at[1] + 1]
+            return state * d + m[0:head]
+
+        reply(blocks - 1, lax.fori_loop(0, blocks - 1, step, jnp.zeros((head, nstate), F32)))
         inc[l, s, me] = inco[l, s, me]
 
     def back(l, s):
         def arrive(b, _):
-            @pl.when(b != me)
+            @pl.when((b != me) & (me > 0))
             def _():
                 reply_arrival(l, s, b).wait_recv()
 
@@ -454,8 +462,8 @@
         for l in range(2):
             for s in range(seqs):
                 peer = lax.rem(me + k, blocks)
-                state_copy(l, s, peer).wait_send()
-                reply_copy(l, s, peer).wait_send()
+                pl.when(me < blocks - 1)(state_copy(l, s, peer).wait_send)
+                pl.when(peer > 0)(reply_copy(l, s, peer).wait_send)
         return 0
 
     lax.fori_loop(1, blocks, drain, 0)

time: 64.1 us -> 63.5 us (level)
  no operation moved by 1% of the time
where the time goes in v4:
time: 63.5 us; the launch traced here: 62.9 us
  Pallas kernels  61.9 us (97%)
  local copies, waits for them, and re-layouts  0.97 us (2%)
    pallas_call x1, Pallas kernels, shards(): pl.pallas_call(functools.partial(kernel, blocks), out_shape=jax.ShapeDtyp...  61.9 us

profile of v4, /device:TPU:249, one launch (start us, length us, event | category | flops | bytes accessed | tf_op | source)
XLA Modules:
  0.0 62.9 jit_solution(3921652759155456269)
XLA Ops:
  0.0 61.9 %shard_map.109 = bf16[1,2,256,1024]{3,2,1,0:T(8,128)(2,1)S(1)} custom-call(bf16[2,256,1024]{2,1,0:T(8,128)(2,1)} %emb.1, bf16[1,1024,2304]{2,1,0:T(8,128)(2,1)} %wide.1, bf16[1,32,1024]{2,1,0:T(8,128)(2,1)} %bitcast.1, f32[1,4,2304]{2,1,0:T(4,128)} %taps.1, f32[1,2304]{1,0:T(1,128)} %tbias.1, f32[1,32]{1,0:T(1,128)} %sbias.1, f32[1,32]{1,0:T(1,128)} %dlog.1, ...), custom_call_target="tpu_custom_call" | custom-call | tf_op jit(solution)/shard_map/pallas_call | solution.py:488
  62.0 1.0 %copy.13 = bf16[1,2,256,1024]{3,2,1,0:T(8,128)(2,1)} copy(bf16[1,2,256,1024]{3,2,1,0:T(8,128)(2,1)S(1)} %shard_map.109) | data formatting | bytes 2097152

commit v5 on v4

--- a/solution.py
+++ b/solution.py
@@ -130,10 +130,11 @@
     def mine(row):
         return jnp.where(core == 0, row[:, 0:heads], row[:, heads : 2 * heads])
 
-    def halo_copy(s, peer):
-        return pltpu.make_async_remote_copy(
-            src_ref=xs.at[1, s, pl.ds(tokens, 8), :], dst_ref=halo.at[s],
-            send_sem=hsend.at[s], recv_sem=hrecv.at[s],
+    def halo_copy(s, peer, i):
+        at = pl.ds(*((0, 3 * cols), (3 * cols, half + bc - 3 * cols))[i])
+        return pltpu.make_async_remote_copy(
+            src_ref=xs.at[1, s, pl.ds(tokens, 8), at], dst_ref=halo.at[s, :, at],
+            send_sem=hsend.at[s, i], recv_sem=hrecv.at[s, i],
             device_id={"block": peer}, device_id_type=MESH,
         )
 
@@ -244,10 +245,10 @@
         normed = normalize(1, h[1, s])
         for lo in range(0, half + bc, cols):
             xs[1, s, 8 : 8 + tokens, lo : lo + cols] = dot(normed, win[1, :, lo : lo + cols])
-
-        @pl.when(me < blocks - 1)
-        def _():
-            halo_copy(s, me + 1).start()
+            if lo == 2 * cols:
+                pl.when(me < blocks - 1)(halo_copy(s, me + 1, 0).start)
+
+        pl.when(me < blocks - 1)(halo_copy(s, me + 1, 1).start)
 
         rates(1, s, normed)
 
@@ -268,7 +269,8 @@
         if l == 1:
             @pl.when(me > 0)
             def _():
-                halo_copy(s, me).wait_recv()
+                for i in range(2):
+                    halo_copy(s, me, i).wait_recv()
                 xs[1, s, 0:8, :] = halo[s]
 
             @pl.when(me == 0)
@@ -451,7 +453,8 @@
     def _():
         edge_copy(me + 1).wait_send()
         for s in range(seqs):
-            halo_copy(s, me + 1).wait_send()
+            for i in range(2):
+                halo_copy(s, me + 1, i).wait_send()
 
     for s in range(seqs):
         for i in range(width // cols):
@@ -524,7 +527,7 @@
             V((2, seqs, tokens, width + 128), BF16),
             V((2, seqs, tokens, width + 128), BF16),
             dma((moved + 1,)), dma((moved,)), dma((moved,)), dma(()), dma(()),
-            dma((seqs,)), dma((seqs,)),
+            dma((seqs, 2)), dma((seqs, 2)),
             dma((2, seqs, blocks)), dma((2, seqs, blocks)),
             dma((2, seqs, blocks)), dma((2, seqs, blocks)),
             dma((2, seqs, width // 256)), dma((2, seqs, width // 256)),

time: 63.5 us -> 63.3 us (level)
  no operation moved by 1% of the time
where the time goes in v5:
time: 63.3 us; the launch traced here: 63.2 us
  Pallas kernels  62.2 us (98%)
  local copies, waits for them, and re-layouts  0.97 us (2%)
    pallas_call x1, Pallas kernels, shards(): pl.pallas_call(functools.partial(kernel, blocks), out_shape=jax.ShapeDtyp...  62.2 us

profile of v5, /device:TPU:249, one launch (start us, length us, event | category | flops | bytes accessed | tf_op | source)
XLA Modules:
  0.0 63.2 jit_solution(2563079669082482894)
XLA Ops:
  0.0 62.2 %shard_map.109 = bf16[1,2,256,1024]{3,2,1,0:T(8,128)(2,1)S(1)} custom-call(bf16[2,256,1024]{2,1,0:T(8,128)(2,1)} %emb.1, bf16[1,1024,2304]{2,1,0:T(8,128)(2,1)} %wide.1, bf16[1,32,1024]{2,1,0:T(8,128)(2,1)} %bitcast.1, f32[1,4,2304]{2,1,0:T(4,128)} %taps.1, f32[1,2304]{1,0:T(1,128)} %tbias.1, f32[1,32]{1,0:T(1,128)} %sbias.1, f32[1,32]{1,0:T(1,128)} %dlog.1, ...), custom_call_target="tpu_custom_call" | custom-call | tf_op jit(solution)/shard_map/pallas_call | solution.py:491
  62.2 1.0 %copy.13 = bf16[1,2,256,1024]{3,2,1,0:T(8,128)(2,1)} copy(bf16[1,2,256,1024]{3,2,1,0:T(8,128)(2,1)S(1)} %shard_map.109) | data formatting | bytes 2097152
